TPU v7x, 32 devices: a whole 2x2x4 slice. The times are simulated.
32 devices in a mesh: grp: 2 (over x), tm: 16 (over z, y, core).
Axes of the slice: x: 2, y: 2, z: 4, core: 2. Of those that a mesh axis runs over, the one named last changes fastest.
Arguments:
- observations: bfloat16 [65536, 1024], P(('grp', 'tm')), parts along dimension 0, may hold values from -0.1875 to 0.1875
- counts: int32 [32], P(('grp', 'tm')), parts along dimension 0, may hold values from 1 to 2048, 10922 in all
- prior: float32 [32, 1024], P(('grp', 'tm')), parts along dimension 0, may hold values from 0.5 to 4
Outputs:
- factors: float32 [32, 1024, 1024], P(('grp', 'tm')), parts along dimension 0
There are 2 independent parts, one for each index of `grp`. A program takes and returns all parts, laid end to end along the dimension named above; each array names one. Nothing has to cross between parts.
Inputs may be any that keep to these rules, and one draw needn't show every extreme that they name: `counts`: some step has exactly 2048 live rows in every draw.
All inputs are finite; a program needn't handle non-finite values. No bound on the sum of `counts` on one device may be relied on, other than what follows from the above.
Results may differ from a plain program's by a relative error of at most 0.0003.
Values sent between devices are 32-bit elements; how exact they have to be, the bound alone decides.
No kernel may reach another device: no remote copies, remote signals or barrier semaphores. Data moves between devices by JAX's collectives and lax.ppermute only.
A program may use at most 64 MiB of HBM per device.

v0:
```python
import jax
import jax.numpy as jnp
from jax import lax
from jax.sharding import PartitionSpec as P


def from_behind(block, axis, distance):
    devices = range(lax.axis_size(axis))
    route = [(i - distance, i) for i in devices if i - distance in devices]
    return lax.ppermute(block, axis, route)


def row_gram(block_rows):
    return lax.dot_general(
        block_rows, block_rows, (((0,), (0,)), ((), ())), preferred_element_type=jnp.float32
    )


def square_back(lower_factor):
    return lax.dot_general(
        lower_factor,
        lower_factor,
        (((1,), (1,)), ((), ())),
        precision=lax.Precision.HIGHEST,
        preferred_element_type=jnp.float32,
    )


def split_cholesky(matrix):
    order = matrix.shape[0]
    half = order // 2
    lead_block = jnp.linalg.cholesky(matrix[:half, :half])
    side_block = jax.scipy.linalg.solve_triangular(lead_block, matrix[half:, :half].T, lower=True).T
    trailing = matrix[half:, half:] - square_back(side_block)
    tail_block = jnp.linalg.cholesky(trailing)
    upper_rows = jnp.concatenate([lead_block, jnp.zeros((half, order - half), matrix.dtype)], 1)
    lower_rows = jnp.concatenate([side_block, tail_block], 1)
    return jnp.concatenate([upper_rows, lower_rows], 0)


def body(observations, counts, prior):
    capacity, columns = observations.shape
    live_count = counts[0]
    row_index = lax.broadcasted_iota(jnp.int32, (capacity, 1), 0)
    masked = jnp.where(row_index < live_count, observations, jnp.zeros_like(observations))
    gram_matrix = row_gram(masked)
    gram_matrix = gram_matrix + jnp.diag(prior[0])
    level_one = gram_matrix + from_behind(gram_matrix, "tm", 1)
    level_two = level_one + from_behind(level_one, "tm", 2)
    upper_factor = split_cholesky(level_two).T
    return upper_factor[None]


def solution(mesh):
    placed = (P(("grp", "tm"), None), P(("grp", "tm")), P(("grp", "tm"), None))
    return jax.shard_map(
        body, mesh=mesh, in_specs=placed, out_specs=P(("grp", "tm"), None, None), check_vma=False
    )
```

profile of v0, /device:TPU:0, one launch (start us, length us, event | category | flops | bytes accessed | tf_op | source)
XLA Modules:
  0.0 416.7 jit_solution(13306791997504786718)
XLA Ops:
  0.7 8.5 %select_add_fusion = f32[1024,1024]{0,1:T(8,128)S(1)} fusion(f32[1024]{0:T(1024)} %bitcast.76, bf16[2048,1024]{1,0:T(8,128)(2,1)} %param.4, pred[2048]{0:T(1024)(128)(4,1)S(1)} %iota_compare_fusion.5), kind=kOutput, calls=%fused_computation.5 | convolution fusion | flops 4300210176 | bytes 8394752 | tf_op jit(solution)/shard_map/dot_general | solution.py:14
  11.9 6.5 %collective-permute-done = f32[1024,1024]{0,1:T(8,128)S(1)} collective-permute-done((f32[1024,1024]{0,1:T(8,128)S(1)}, f32[1024,1024]{0,1:T(8,128)S(1)}, u32[]{:S(2)}, u32[]{:S(2)}) %collective-permute-start) | collective-permute-done | bytes 4194336 | tf_op jit(solution)/shard_map/ppermute | solution.py:10
  18.4 2.9 add.45
  21.3 47.7 %collective-permute-start.1 = (f32[1024,1024]{0,1:T(8,128)}, f32[1024,1024]{0,1:T(8,128)}, u32[]{:S(2)}, u32[]{:S(2)}) collective-permute-start(f32[1024,1024]{0,1:T(8,128)} %add.45), channel_id=1, source_target_pairs={{0,2},{1,3},{2,4},{3,5},{4,6},{5,7},{6,8},{7,9},{8,10},{9,11},{10,... | collective-permute-start | bytes 12582920 | tf_op jit(solution)/shard_map/ppermute | solution.py:10
  69.0 87.3 %collective-permute-done.1 = f32[1024,1024]{0,1:T(8,128)} collective-permute-done((f32[1024,1024]{0,1:T(8,128)}, f32[1024,1024]{0,1:T(8,128)}, u32[]{:S(2)}, u32[]{:S(2)}) %collective-permute-start.1) | collective-permute-done | bytes 4194336 | tf_op jit(solution)/shard_map/ppermute | solution.py:10
  156.3 4.4 %add.46 = f32[1024,1024]{0,1:T(8,128)S(1)} add(f32[1024,1024]{0,1:T(8,128)} %add.45, f32[1024,1024]{0,1:T(8,128)} %collective-permute-done.1) | non-fusion elementwise | flops 1048576 | bytes 12582912 | tf_op jit(solution)/shard_map/add | solution.py:49
  164.7 11.7 %cholesky.286 = f32[128,128]{1,0:T(8,128)S(1)} custom-call(f32[128,128]{1,0:T(8,128)S(1)} %cholesky.426), custom_call_target="Cholesky" | custom-call | tf_op jit(solution)/shard_map/jit(cholesky)/cholesky | solution.py:32
  176.5 9.8 %custom-call.28 = f32[1,128,128]{1,2,0:T(8,128)S(1)} custom-call(f32[1,128,128]{2,1,0:T(8,128)S(1)} %get-tuple-element.47), custom_call_target="InvertDiagBlocksLowerTriangular" | custom-call | tf_op jit(solution)/shard_map/jit(cholesky)/cholesky | solution.py:32
  187.1 12.2 %cholesky.305 = f32[128,128]{1,0:T(8,128)S(1)} custom-call(f32[128,128]{1,0:T(8,128)S(1)} %cholesky.430), custom_call_target="Cholesky" | custom-call | tf_op jit(solution)/shard_map/jit(cholesky)/cholesky | solution.py:32
  199.3 9.8 %custom-call.29 = f32[1,128,128]{1,2,0:T(8,128)S(1)} custom-call(f32[1,128,128]{2,1,0:T(8,128)S(1)} %get-tuple-element.44), custom_call_target="InvertDiagBlocksLowerTriangular" | custom-call | tf_op jit(solution)/shard_map/jit(cholesky)/cholesky | solution.py:32
  209.8 11.7 %cholesky.326 = f32[128,128]{1,0:T(8,128)S(1)} custom-call(f32[128,128]{1,0:T(8,128)S(1)} %cholesky.435), custom_call_target="Cholesky" | custom-call | tf_op jit(solution)/shard_map/jit(cholesky)/cholesky | solution.py:32
  222.2 9.8 %custom-call.30 = f32[1,128,128]{1,2,0:T(8,128)S(1)} custom-call(f32[1,128,128]{2,1,0:T(8,128)S(1)} %get-tuple-element.41), custom_call_target="InvertDiagBlocksLowerTriangular" | custom-call | tf_op jit(solution)/shard_map/jit(cholesky)/cholesky | solution.py:32
  232.6 11.9 %cholesky.343 = f32[128,128]{1,0:T(8,128)S(1)} custom-call(f32[128,128]{1,0:T(8,128)S(1)} %convolution_subtract_fusion.5), custom_call_target="Cholesky" | custom-call | tf_op jit(solution)/shard_map/jit(cholesky)/cholesky | solution.py:32
  249.7 14.1 %while.1 = (s32[]{:T(128)}, f32[512,512]{1,0:T(8,128)}, s32[4,2]{0,1:T(2,128)S(1)}, f32[4,128,128]{2,1,0:T(8,128)}, s32[]{:T(128)}) while((s32[]{:T(128)}, f32[512,512]{1,0:T(8,128)}, s32[4,2]{0,1:T(2,128)S(1)}, f32[4,128,128]{2,1,0:T(8,128)}, s32[]{:T(128)}) %tuple.36), condition=%wide.while_cond, body=%wide.while_body.sunk | while | flops 2 | bytes 132705 | solution.py:33
  263.8 40.1 %custom-call.24 = f32[4,128,128]{1,2,0:T(8,128)S(1)} custom-call(f32[4,128,128]{2,1,0:T(8,128)} %get-tuple-element.13), custom_call_target="InvertDiagBlocksLowerTriangular" | custom-call | tf_op jit(solution)/shard_map/jit(_solve_triangular)/triangular_solve | solution.py:33
  311.3 3.4 slice_subtract_fusion
  318.5 11.7 %cholesky.358 = f32[128,128]{1,0:T(8,128)S(1)} custom-call(f32[128,128]{1,0:T(8,128)S(1)} %cholesky.439), custom_call_target="Cholesky" | custom-call | tf_op jit(solution)/shard_map/jit(cholesky)/cholesky | solution.py:35
  330.4 9.8 %custom-call.31 = f32[1,128,128]{1,2,0:T(8,128)S(1)} custom-call(f32[1,128,128]{2,1,0:T(8,128)S(1)} %get-tuple-element.37), custom_call_target="InvertDiagBlocksLowerTriangular" | custom-call | tf_op jit(solution)/shard_map/jit(cholesky)/cholesky | solution.py:35
  344.0 11.7 %cholesky.377 = f32[128,128]{1,0:T(8,128)S(1)} custom-call(f32[128,128]{1,0:T(8,128)S(1)} %cholesky.443), custom_call_target="Cholesky" | custom-call | tf_op jit(solution)/shard_map/jit(cholesky)/cholesky | solution.py:35
  357.1 9.8 %custom-call.32 = f32[1,128,128]{1,2,0:T(8,128)S(1)} custom-call(f32[1,128,128]{2,1,0:T(8,128)S(1)} %get-tuple-element.34), custom_call_target="InvertDiagBlocksLowerTriangular" | custom-call | tf_op jit(solution)/shard_map/jit(cholesky)/cholesky | solution.py:35
  369.4 11.7 %cholesky.398 = f32[128,128]{1,0:T(8,128)S(1)} custom-call(f32[128,128]{1,0:T(8,128)S(1)} %cholesky.448), custom_call_target="Cholesky" | custom-call | tf_op jit(solution)/shard_map/jit(cholesky)/cholesky | solution.py:35
  381.9 10.0 %custom-call.33 = f32[1,128,128]{1,2,0:T(8,128)S(1)} custom-call(f32[1,128,128]{2,1,0:T(8,128)S(1)} %get-tuple-element.31), custom_call_target="InvertDiagBlocksLowerTriangular" | custom-call | tf_op jit(solution)/shard_map/jit(cholesky)/cholesky | solution.py:35
  393.4 11.7 %cholesky.415 = f32[128,128]{1,0:T(8,128)S(1)} custom-call(f32[128,128]{1,0:T(8,128)S(1)} %convolution_subtract_fusion.4), custom_call_target="Cholesky" | custom-call | tf_op jit(solution)/shard_map/jit(cholesky)/cholesky | solution.py:35
  410.9 5.3 %copy.15 = f32[1,1024,1024]{2,1,0:T(8,128)} copy(f32[1,1024,1024]{1,2,0:T(8,128)} %fusion) | data formatting | bytes 8388608 | tf_op jit(solution)/shard_map/broadcast_in_dim | solution.py:51
  (85 shorter events, 50.2 us)
Async XLA Ops:
  9.2 9.2 %collective-permute-start = (f32[1024,1024]{0,1:T(8,128)S(1)}, f32[1024,1024]{0,1:T(8,128)S(1)}, u32[]{:S(2)}, u32[]{:S(2)}) collective-permute-start(f32[1024,1024]{0,1:T(8,128)S(1)} %select_add_fusion), channel_id=1, source_target_pairs={{0,1},{1,2},{2,3},{3,4},{4,5},{5,6},{6,7},{7,8},{8,9},{9,10},{10,1... | collective-permute-start | bytes 12582920 | tf_op jit(solution)/shard_map/ppermute | solution.py:10
  21.3 135.0 %collective-permute-start.1 = (f32[1024,1024]{0,1:T(8,128)}, f32[1024,1024]{0,1:T(8,128)}, u32[]{:S(2)}, u32[]{:S(2)}) collective-permute-start(f32[1024,1024]{0,1:T(8,128)} %add.45), channel_id=1, source_target_pairs={{0,2},{1,3},{2,4},{3,5},{4,6},{5,7},{6,8},{7,9},{8,10},{9,11},{10,... | collective-permute-start | bytes 12582920 | tf_op jit(solution)/shard_map/ppermute | solution.py:10
  160.7 2.0 copy-start
  303.9 3.8 copy-start.5
  309.6 1.6 copy-start.2
  309.7 1.5 copy-start.3
  317.5 1.0 copy-start.1
  343.3 0.7 copy-start.4
where the time goes:
time: 423 us; the launch traced here: 417 us
  other arithmetic  213 us (50%)
  waiting for transfers between devices  93.8 us (22%)
  starting transfers between devices  50.3 us (12%)
  matrix products  27.3 us (6%)
  local copies, waits for them, and re-layouts  25.7 us (6%)
  between operations  6.88 us (2%)
    ppermute x2, waiting for transfers between devices, from_behind(): return lax.ppermute(block, axis, route)  93.8 us
    another operation x15, other arithmetic, split_cholesky(): tail_block = jnp.linalg.cholesky(trailing)  79.4 us
    another operation x14, other arithmetic, split_cholesky(): lead_block = jnp.linalg.cholesky(matrix[:half, :half])  79.1 us
    ppermute x2, starting transfers between devices, from_behind(): return lax.ppermute(block, axis, route)  50.3 us
    another operation x3, other arithmetic, split_cholesky(): jax.scipy.linalg.solve_triangular(lead_block, matrix[half:, :half].T, low...  41.4 us
    another operation x12, local copies, waits for them, and re-layouts  14.1 us
    dot_general x1, matrix products, row_gram(): lax.dot_general(block_rows, block_rows, (((0,), (0,)), ((), ())), preferr...  8.52 us
  transfers between devices with their start and end apart: 2, of which 2 were waited for; matrix products, arithmetic and copies ran while one was open for 0% of the time, Pallas kernels for 0%

commit v1 on v0

v1 whole, which is shorter than its diff:
```python
import functools
import jax
import jax.numpy as jnp
from jax import lax
from jax.experimental import pallas as pl
from jax.experimental.pallas import tpu as pltpu
from jax.sharding import PartitionSpec as P

LANES = 128
SUBS = 8
MICRO = 32
ROWS = 256
DEPTH = 512
FULL = lax.Precision.HIGHEST


def dot_tn(a, b):
    return lax.dot_general(a, b, (((0,), (0,)), ((), ())), precision=FULL, preferred_element_type=jnp.float32)


def dot_nn(a, b):
    return lax.dot_general(a, b, (((1,), (0,)), ((), ())), precision=FULL, preferred_element_type=jnp.float32)


def row_of(x, i):
    return jnp.broadcast_to(x[i:i + 1, :], x.shape)


def lane_of(x, j):
    return jnp.broadcast_to(x[:, j:j + 1], x.shape)


def eliminate(tiles, first):
    sub = lax.broadcasted_iota(jnp.int32, (SUBS, LANES), 0)
    groups = len(tiles)
    for p in range(groups):
        cols = [[lane_of(tiles[g][0], first + SUBS * p + j) for g in range(p, groups)] for j in range(SUBS)]
        scale = None
        for i in range(SUBS):
            pivot = row_of(cols[i][0], i)
            inv = 1.0 / pivot
            root = lax.rsqrt(pivot)
            scale = root if scale is None else jnp.where(sub == i, root, scale)
            mult = [c * inv for c in cols[i]]
            mult[0] = jnp.where(sub > i, mult[0], 0.0)
            for j in range(i + 1, SUBS):
                e = row_of(cols[j][0], i)
                cols[j] = [c - m * e for c, m in zip(cols[j], mult)]
            for t in range(len(tiles[p])):
                e = row_of(tiles[p][t], i)
                for g in range(p, groups):
                    tiles[g][t] = tiles[g][t] - mult[g - p] * e
        tiles[p] = [t * scale for t in tiles[p]]
    return tiles


def factor_diag(d_ref):
    n = d_ref.shape[0]
    for r0 in range(0, n, MICRO):
        tiles = [[d_ref[r0 + SUBS * g:r0 + SUBS * (g + 1), LANES * t:LANES * (t + 1)] for t in range(2)] for g in range(MICRO // SUBS)]
        tiles = eliminate(tiles, r0)
        for g, row in enumerate(tiles):
            for t, tile in enumerate(row):
                d_ref[r0 + SUBS * g:r0 + SUBS * (g + 1), LANES * t:LANES * (t + 1)] = tile
        r1 = r0 + MICRO
        if r1 < n:
            u = d_ref[r0:r1, :]
            d_ref[r1:, :] = d_ref[r1:, :] - dot_tn(u[:, :LANES], u)[r1:]


def chunk_kernel(start, n_parts, *refs):
    parts = refs[:n_parts]
    refs = refs[n_parts:]
    if start:
        prev_ref, out_ref, a_ref, d_ref, o_ref, u_ref, sem = refs
    else:
        out_ref, a_ref, d_ref, o_ref, sem = refs
    rows, width = a_ref.shape
    size = start + width
    if start:
        fetch = pltpu.make_async_copy(prev_ref.at[pl.ds(0, start), pl.ds(start, width)], u_ref, sem.at[0])
        fetch.start()
    total = parts[0][...]
    for p in parts[1:]:
        total = total + p[...]
    if start:
        fetch.wait()
        total = total - dot_tn(u_ref[:, :rows], u_ref[...])
    a_ref[...] = total
    o_ref[...] = jnp.zeros_like(o_ref)
    r = lax.broadcasted_iota(jnp.int32, (LANES, LANES), 0)
    c = lax.broadcasted_iota(jnp.int32, (LANES, LANES), 1)
    eye = jnp.where(r == c, 1.0, 0.0).astype(jnp.float32)
    for b in range(0, rows, LANES):
        e = b + LANES
        d_ref[:, :LANES] = a_ref[b:e, b:e]
        d_ref[:, LANES:] = eye
        factor_diag(d_ref)
        o_ref[b:e, start + b:start + e] = jnp.where(r <= c, d_ref[:, :LANES], 0.0)
        if e < width:
            u = dot_nn(d_ref[:, LANES:], a_ref[b:e, e:])
            o_ref[b:e, start + e:] = u
            if e < rows:
                a_ref[e:, e:] = a_ref[e:, e:] - dot_tn(u[:, :rows - e], u)
    put = pltpu.make_async_copy(o_ref, out_ref.at[pl.ds(start, rows), :], sem.at[1])
    put.start()
    put.wait()


def factor_rows(start, rows, size, parts, prev):
    width = size - start
    f32 = jnp.float32
    scratch = [pltpu.VMEM((rows, width), f32), pltpu.VMEM((LANES, 2 * LANES), f32), pltpu.VMEM((rows, size), f32)]
    in_specs = [pl.BlockSpec(memory_space=pltpu.VMEM)] * len(parts)
    args = list(parts)
    aliases = {}
    if start:
        in_specs.append(pl.BlockSpec(memory_space=pl.ANY))
        args.append(prev)
        aliases = {len(parts): 0}
        scratch.append(pltpu.VMEM((start, width), f32))
    scratch.append(pltpu.SemaphoreType.DMA((2,)))
    return pl.pallas_call(
        functools.partial(chunk_kernel, start, len(parts)),
        out_shape=jax.ShapeDtypeStruct((size, size), f32),
        in_specs=in_specs,
        out_specs=pl.BlockSpec(memory_space=pl.ANY),
        scratch_shapes=scratch,
        input_output_aliases=aliases,
        name=f"factor_{start}",
    )(*args)


def gram_kernel(count_ref, h_ref, prior_ref, out_ref):
    k = pl.program_id(0)
    depth = h_ref.shape[0]
    rows, width = out_ref.shape
    start = h_ref.shape[1] - width
    left = count_ref[0] - k * depth

    @pl.when(k == 0)
    def _():
        r = lax.broadcasted_iota(jnp.int32, (rows, rows), 0)
        c = lax.broadcasted_iota(jnp.int32, (rows, rows), 1)
        out_ref[:, :rows] = jnp.where(r == c, jnp.broadcast_to(prior_ref[:, start:start + rows], (rows, rows)), 0.0)
        if width > rows:
            out_ref[:, rows:] = jnp.zeros((rows, width - rows), jnp.float32)

    @pl.when(left > 0)
    def _():
        index = lax.broadcasted_iota(jnp.int32, h_ref.shape, 0)
        h = jnp.where(index < left, h_ref[...], jnp.zeros_like(h_ref))[:, start:]
        out_ref[...] += lax.dot_general(h[:, :rows], h, (((0,), (0,)), ((), ())), preferred_element_type=jnp.float32)


def gram_rows(start, rows, observations, counts, prior):
    capacity, size = observations.shape
    depth = min(DEPTH, capacity)
    width = size - start

    def block(k, count):
        return jnp.minimum(k, (count[0] - 1) // depth), 0

    grid_spec = pltpu.PrefetchScalarGridSpec(
        num_scalar_prefetch=1,
        grid=(capacity // depth,),
        in_specs=[
            pl.BlockSpec((depth, size), block),
            pl.BlockSpec((1, size), lambda k, count: (0, 0)),
        ],
        out_specs=pl.BlockSpec((rows, width), lambda k, count: (0, 0)),
    )
    return pl.pallas_call(
        gram_kernel,
        out_shape=jax.ShapeDtypeStruct((rows, width), jnp.float32),
        grid_spec=grid_spec,
        name=f"gram_{start}",
    )(counts, observations, prior)


def from_behind(block, axis, distance):
    devices = range(lax.axis_size(axis))
    route = [(i - distance, i) for i in devices if i - distance in devices]
    return lax.ppermute(block, axis, route)


def body(observations, counts, prior):
    size = observations.shape[1]
    starts = range(0, size, ROWS)
    parts = []
    for start in starts:
        gram = gram_rows(start, ROWS, observations, counts, prior)
        level_one = gram + from_behind(gram, "tm", 1)
        parts.append([level_one, from_behind(level_one, "tm", 2)])
    factor = None
    for start, part in zip(starts, parts):
        factor = factor_rows(start, ROWS, size, part, factor)
    return factor[None]


def solution(mesh):
    placed = (P(("grp", "tm"), None), P(("grp", "tm")), P(("grp", "tm"), None))
    return jax.shard_map(
        body, mesh=mesh, in_specs=placed, out_specs=P(("grp", "tm"), None, None), check_vma=False
    )
```

time: 423 us -> 146 us (0.35); the launches traced: 417 us -> 145 us
  other arithmetic: 213 us -> 4.69 us
  waiting for transfers between devices: 93.8 us -> 0.02 us
  Pallas kernels: 0 us -> 65.4 us
  matrix products: 27.3 us -> 0 us
  local copies, waits for them, and re-layouts: 25.7 us -> 1.5 us
  starting transfers between devices: 50.3 us -> 72.7 us
  between operations: 6.88 us -> 1.03 us
    another operation x32 -> x0, other arithmetic: 200 us -> none  [the longest x15 79.4 us: split_cholesky(): tail_block = jnp.linalg.cholesky(trailing)]
    ppermute x2 -> x8, waiting for transfers between devices: 93.8 us -> 0.02 us  [from_behind(): return lax.ppermute(block, axis, route)]
    pallas_call x0 -> x8, Pallas kernels: none -> 65.4 us  [the longest x4 53.5 us: factor_rows(): pl.pallas_call(functools.partial(chunk_kernel, start, len(parts)), out_sh...]
    ppermute x2 -> x8, starting transfers between devices: 50.3 us -> 72.7 us  [from_behind(): return lax.ppermute(block, axis, route)]
    another operation x19 -> x0, matrix products: 15.3 us -> none  [the longest x7 6.82 us: split_cholesky(): jax.scipy.linalg.solve_triangular(lead_block, matrix[half:, :half].T, low...]
    another operation x26 -> x0, local copies, waits for them, and re-layouts: 14.9 us -> none
    dot_general x2 -> x0, matrix products: 11.9 us -> none  [the longest x1 8.52 us: row_gram(): lax.dot_general(block_rows, block_rows, (((0,), (0,)), ((), ())), preferr...]
    broadcast_in_dim x1 -> x0, local copies, waits for them, and re-layouts: 5.34 us -> none  [body(): return upper_factor[None]]
  transfers between devices with their start and end apart: 2 -> 8, of which waited for: 2 -> 0; matrix products, arithmetic and copies ran while one was open for 0% -> 3% of each run, Pallas kernels for 0% -> 33%
where the time goes in v1:
time: 146 us; the launch traced here: 145 us
  starting transfers between devices  72.7 us (50%)
  Pallas kernels  65.4 us (45%)
  other arithmetic  4.69 us (3%)
  local copies, waits for them, and re-layouts  1.5 us (1%)
    ppermute x8, starting transfers between devices, from_behind(): return lax.ppermute(block, axis, route)  72.7 us
    pallas_call x4, Pallas kernels, factor_rows(): pl.pallas_call(functools.partial(chunk_kernel, start, len(parts)), out_sh...  53.5 us
    pallas_call x4, Pallas kernels, gram_rows(): pl.pallas_call(gram_kernel, out_shape=jax.ShapeDtypeStruct((rows, width),...  11.9 us
    add x4, other arithmetic, body(): level_one = gram + from_behind(gram, 'tm', 1)  4.69 us
  transfers between devices with their start and end apart: 8, of which 0 were waited for; matrix products, arithmetic and copies ran while one was open for 3% of the time, Pallas kernels for 33%

profile of v1, /device:TPU:0, one launch (start us, length us, event | category | flops | bytes accessed | tf_op | source)
XLA Modules:
  0.0 145.3 jit_solution(11994565563150790091)
XLA Ops:
  0.7 3.3 %gram_0.1 = f32[256,1024]{1,0:T(8,128)} custom-call(s32[1]{0:T(128)S(6)} %copy.10.count_ref, bf16[2048,1024]{1,0:T(8,128)(2,1)} %h_ref.7, f32[1,1024]{1,0:T(1,128)} %prior_ref.7), custom_call_target="tpu_custom_call" | custom-call | tf_op jit(solution)/shard_map/gram_0/pallas_call | solution.py:173
  4.0 3.0 %collective-permute-start.6 = (f32[256,1024]{1,0:T(8,128)}, f32[256,1024]{1,0:T(8,128)}, u32[]{:S(2)}, u32[]{:S(2)}) collective-permute-start(f32[256,1024]{1,0:T(8,128)} %gram_0.1), channel_id=1, source_target_pairs={{0,1},{1,2},{2,3},{3,4},{4,5},{5,6},{6,7},{7,8},{8,9},{9,10},{10,1... | collective-permute-start | bytes 3145736 | tf_op jit(solution)/shard_map/ppermute | solution.py:184
  7.0 3.1 %gram_256.1 = f32[256,768]{1,0:T(8,128)} custom-call(s32[1]{0:T(128)S(6)} %copy.10.count_ref, bf16[2048,1024]{1,0:T(8,128)(2,1)} %h_ref.7, f32[1,1024]{1,0:T(1,128)} %prior_ref.7), custom_call_target="tpu_custom_call" | custom-call | tf_op jit(solution)/shard_map/gram_256/pallas_call | solution.py:173
  10.2 6.4 %collective-permute-start.4 = (f32[256,768]{1,0:T(8,128)}, f32[256,768]{1,0:T(8,128)}, u32[]{:S(2)}, u32[]{:S(2)}) collective-permute-start(f32[256,768]{1,0:T(8,128)} %gram_256.1), channel_id=1, source_target_pairs={{0,1},{1,2},{2,3},{3,4},{4,5},{5,6},{6,7},{7,8},{8,9},{9,10},{10,1... | collective-permute-start | bytes 2359304 | tf_op jit(solution)/shard_map/ppermute | solution.py:184
  16.5 0.0 collective-permute-done.6
  16.5 1.4 add.15.refs_0_
  17.9 11.7 %collective-permute-start.7 = (f32[256,1024]{1,0:T(8,128)S(1)}, f32[256,1024]{1,0:T(8,128)}, u32[]{:S(2)}, u32[]{:S(2)}) collective-permute-start(f32[256,1024]{1,0:T(8,128)S(1)} %add.15.refs_0_), channel_id=1, source_target_pairs={{0,2},{1,3},{2,4},{3,5},{4,6},{5,7},{6,8},{7,9},{8,10},{9,11},{10,... | collective-permute-start | bytes 3145736 | tf_op jit(solution)/shard_map/ppermute | solution.py:184
  29.5 2.8 %gram_512.1 = f32[256,512]{1,0:T(8,128)} custom-call(s32[1]{0:T(128)S(6)} %copy.10.count_ref, bf16[2048,1024]{1,0:T(8,128)(2,1)} %h_ref.7, f32[1,1024]{1,0:T(1,128)} %prior_ref.7), custom_call_target="tpu_custom_call" | custom-call | tf_op jit(solution)/shard_map/gram_512/pallas_call | solution.py:173
  32.4 2.2 %collective-permute-start.2 = (f32[256,512]{1,0:T(8,128)}, f32[256,512]{1,0:T(8,128)}, u32[]{:S(2)}, u32[]{:S(2)}) collective-permute-start(f32[256,512]{1,0:T(8,128)} %gram_512.1), channel_id=1, source_target_pairs={{0,1},{1,2},{2,3},{3,4},{4,5},{5,6},{6,7},{7,8},{8,9},{9,10},{10,1... | collective-permute-start | bytes 1572872 | tf_op jit(solution)/shard_map/ppermute | solution.py:184
  34.6 0.0 collective-permute-done.4
  34.6 1.2 add.14.refs_0_
  35.9 3.9 %collective-permute-start.5 = (f32[256,768]{1,0:T(8,128)S(1)}, f32[256,768]{1,0:T(8,128)}, u32[]{:S(2)}, u32[]{:S(2)}) collective-permute-start(f32[256,768]{1,0:T(8,128)S(1)} %add.14.refs_0_), channel_id=1, source_target_pairs={{0,2},{1,3},{2,4},{3,5},{4,6},{5,7},{6,8},{7,9},{8,10},{9,11},{10,... | collective-permute-start | bytes 2359304 | tf_op jit(solution)/shard_map/ppermute | solution.py:184
  39.8 2.6 %gram_768.1 = f32[256,256]{1,0:T(8,128)} custom-call(s32[1]{0:T(128)S(6)} %copy.10.count_ref, bf16[2048,1024]{1,0:T(8,128)(2,1)} %h_ref.7, f32[1,1024]{1,0:T(1,128)} %prior_ref.7), custom_call_target="tpu_custom_call" | custom-call | tf_op jit(solution)/shard_map/gram_768/pallas_call | solution.py:173
  42.4 1.3 collective-permute-start
  43.7 1.1 add.13.refs_0_
  44.9 27.1 %collective-permute-start.3 = (f32[256,512]{1,0:T(8,128)S(1)}, f32[256,512]{1,0:T(8,128)S(1)}, u32[]{:S(2)}, u32[]{:S(2)}) collective-permute-start(f32[256,512]{1,0:T(8,128)S(1)} %add.13.refs_0_), channel_id=1, source_target_pairs={{0,2},{1,3},{2,4},{3,5},{4,6},{5,7},{6,8},{7,9},{8,10},{9,11},{10,... | collective-permute-start | bytes 1572872 | tf_op jit(solution)/shard_map/ppermute | solution.py:184
  72.0 1.0 add.12.refs_0_
  73.0 17.1 %collective-permute-start.1 = (f32[256,256]{1,0:T(8,128)S(1)}, f32[256,256]{1,0:T(8,128)S(1)}, u32[]{:S(2)}, u32[]{:S(2)}) collective-permute-start(f32[256,256]{1,0:T(8,128)S(1)} %add.12.refs_0_), channel_id=1, source_target_pairs={{0,2},{1,3},{2,4},{3,5},{4,6},{5,7},{6,8},{7,9},{8,10},{9,11},{10,... | collective-permute-start | bytes 786440 | tf_op jit(solution)/shard_map/ppermute | solution.py:184
  90.1 12.3 %factor_0.1.refs_2_ = f32[1024,1024]{1,0:T(8,128)} custom-call(f32[256,1024]{1,0:T(8,128)} %copy-done, f32[256,1024]{1,0:T(8,128)} %collective-permute-done.7.refs_1_), custom_call_target="tpu_custom_call" | custom-call | tf_op jit(solution)/shard_map/factor_0/pallas_call | solution.py:123
  102.4 13.8 %factor_256.1.refs_2_ = f32[1024,1024]{1,0:T(8,128)} custom-call(f32[256,768]{1,0:T(8,128)} %copy-done.2, f32[256,768]{1,0:T(8,128)} %collective-permute-done.5.refs_1_, f32[1024,1024]{1,0:T(8,128)} %factor_0.1.refs_2_), custom_call_target="tpu_custom_call", output_to_operand_aliasing={{}: (2, {})} | custom-call | tf_op jit(solution)/shard_map/factor_256/pallas_call | solution.py:123
  116.3 0.8 copy-done.7
  117.0 13.9 %factor_512.1.refs_2_ = f32[1024,1024]{1,0:T(8,128)} custom-call(f32[256,512]{1,0:T(8,128)} %copy-done.4, f32[256,512]{1,0:T(8,128)} %copy-done.7, f32[1024,1024]{1,0:T(8,128)} %factor_256.1.refs_2_), custom_call_target="tpu_custom_call", output_to_operand_aliasing={{}: (2, {})} | custom-call | tf_op jit(solution)/shard_map/factor_512/pallas_call | solution.py:123
  131.0 0.7 copy-done.8
  131.7 13.5 %factor_768.1 = f32[1024,1024]{1,0:T(8,128)} custom-call(f32[256,256]{1,0:T(8,128)} %copy-done.6, f32[256,256]{1,0:T(8,128)} %copy-done.8, f32[1024,1024]{1,0:T(8,128)} %factor_512.1.refs_2_), custom_call_target="tpu_custom_call", output_to_operand_aliasing={{}: (2, {})} | custom-call | tf_op jit(solution)/shard_map/factor_768/pallas_call | solution.py:123
  (22 shorter events, 0.0 us)
Async XLA Ops:
  4.0 12.5 %copy-start.1 = (f32[256,1024]{1,0:T(8,128)S(1)}, f32[256,1024]{1,0:T(8,128)}, u32[]{:S(2)}) copy-start(f32[256,1024]{1,0:T(8,128)} %gram_0.1) | copy-start | bytes 3145732
  4.0 12.5 %collective-permute-start.6 = (f32[256,1024]{1,0:T(8,128)}, f32[256,1024]{1,0:T(8,128)}, u32[]{:S(2)}, u32[]{:S(2)}) collective-permute-start(f32[256,1024]{1,0:T(8,128)} %gram_0.1), channel_id=1, source_target_pairs={{0,1},{1,2},{2,3},{3,4},{4,5},{5,6},{6,7},{7,8},{8,9},{9,10},{10,1... | collective-permute-start | bytes 3145736 | tf_op jit(solution)/shard_map/ppermute | solution.py:184
  10.2 24.5 %copy-start.3 = (f32[256,768]{1,0:T(8,128)S(1)}, f32[256,768]{1,0:T(8,128)}, u32[]{:S(2)}) copy-start(f32[256,768]{1,0:T(8,128)} %gram_256.1) | copy-start | bytes 2359300
  10.2 24.5 %collective-permute-start.4 = (f32[256,768]{1,0:T(8,128)}, f32[256,768]{1,0:T(8,128)}, u32[]{:S(2)}, u32[]{:S(2)}) collective-permute-start(f32[256,768]{1,0:T(8,128)} %gram_256.1), channel_id=1, source_target_pairs={{0,1},{1,2},{2,3},{3,4},{4,5},{5,6},{6,7},{7,8},{8,9},{9,10},{10,1... | collective-permute-start | bytes 2359304 | tf_op jit(solution)/shard_map/ppermute | solution.py:184
  17.9 24.5 %copy-start = (f32[256,1024]{1,0:T(8,128)}, f32[256,1024]{1,0:T(8,128)S(1)}, u32[]{:S(2)}) copy-start(f32[256,1024]{1,0:T(8,128)S(1)} %add.15.refs_0_) | copy-start | bytes 3145732
  17.9 72.2 %collective-permute-start.7 = (f32[256,1024]{1,0:T(8,128)S(1)}, f32[256,1024]{1,0:T(8,128)}, u32[]{:S(2)}, u32[]{:S(2)}) collective-permute-start(f32[256,1024]{1,0:T(8,128)S(1)} %add.15.refs_0_), channel_id=1, source_target_pairs={{0,2},{1,3},{2,4},{3,5},{4,6},{5,7},{6,8},{7,9},{8,10},{9,11},{10,... | collective-permute-start | bytes 3145736 | tf_op jit(solution)/shard_map/ppermute | solution.py:184
  32.4 11.3 %copy-start.5 = (f32[256,512]{1,0:T(8,128)S(1)}, f32[256,512]{1,0:T(8,128)}, u32[]{:S(2)}) copy-start(f32[256,512]{1,0:T(8,128)} %gram_512.1) | copy-start | bytes 1572868
  32.4 11.3 %collective-permute-start.2 = (f32[256,512]{1,0:T(8,128)}, f32[256,512]{1,0:T(8,128)}, u32[]{:S(2)}, u32[]{:S(2)}) collective-permute-start(f32[256,512]{1,0:T(8,128)} %gram_512.1), channel_id=1, source_target_pairs={{0,1},{1,2},{2,3},{3,4},{4,5},{5,6},{6,7},{7,8},{8,9},{9,10},{10,1... | collective-permute-start | bytes 1572872 | tf_op jit(solution)/shard_map/ppermute | solution.py:184
  35.8 66.6 %copy-start.2 = (f32[256,768]{1,0:T(8,128)}, f32[256,768]{1,0:T(8,128)S(1)}, u32[]{:S(2)}) copy-start(f32[256,768]{1,0:T(8,128)S(1)} %add.14.refs_0_) | copy-start | bytes 2359300
  35.9 66.6 %collective-permute-start.5 = (f32[256,768]{1,0:T(8,128)S(1)}, f32[256,768]{1,0:T(8,128)}, u32[]{:S(2)}, u32[]{:S(2)}) collective-permute-start(f32[256,768]{1,0:T(8,128)S(1)} %add.14.refs_0_), channel_id=1, source_target_pairs={{0,2},{1,3},{2,4},{3,5},{4,6},{5,7},{6,8},{7,9},{8,10},{9,11},{10,... | collective-permute-start | bytes 2359304 | tf_op jit(solution)/shard_map/ppermute | solution.py:184
  42.4 29.5 %collective-permute-start = (f32[256,256]{1,0:T(8,128)}, f32[256,256]{1,0:T(8,128)S(1)}, u32[]{:S(2)}, u32[]{:S(2)}) collective-permute-start(f32[256,256]{1,0:T(8,128)} %gram_768.1), channel_id=1, source_target_pairs={{0,1},{1,2},{2,3},{3,4},{4,5},{5,6},{6,7},{7,8},{8,9},{9,10},{10,1... | collective-permute-start | bytes 786440 | tf_op jit(solution)/shard_map/ppermute | solution.py:184
  44.9 71.4 %copy-start.4 = (f32[256,512]{1,0:T(8,128)}, f32[256,512]{1,0:T(8,128)S(1)}, u32[]{:S(2)}) copy-start(f32[256,512]{1,0:T(8,128)S(1)} %add.13.refs_0_) | copy-start | bytes 1572868
  44.9 71.4 %collective-permute-start.3 = (f32[256,512]{1,0:T(8,128)S(1)}, f32[256,512]{1,0:T(8,128)S(1)}, u32[]{:S(2)}, u32[]{:S(2)}) collective-permute-start(f32[256,512]{1,0:T(8,128)S(1)} %add.13.refs_0_), channel_id=1, source_target_pairs={{0,2},{1,3},{2,4},{3,5},{4,6},{5,7},{6,8},{7,9},{8,10},{9,11},{10,... | collective-permute-start | bytes 1572872 | tf_op jit(solution)/shard_map/ppermute | solution.py:184
  73.0 43.3 %copy-start.6 = (f32[256,256]{1,0:T(8,128)}, f32[256,256]{1,0:T(8,128)S(1)}, u32[]{:S(2)}) copy-start(f32[256,256]{1,0:T(8,128)S(1)} %add.12.refs_0_) | copy-start | bytes 786436
  73.0 58.0 %collective-permute-start.1 = (f32[256,256]{1,0:T(8,128)S(1)}, f32[256,256]{1,0:T(8,128)S(1)}, u32[]{:S(2)}, u32[]{:S(2)}) collective-permute-start(f32[256,256]{1,0:T(8,128)S(1)} %add.12.refs_0_), channel_id=1, source_target_pairs={{0,2},{1,3},{2,4},{3,5},{4,6},{5,7},{6,8},{7,9},{8,10},{9,11},{10,... | collective-permute-start | bytes 786440 | tf_op jit(solution)/shard_map/ppermute | solution.py:184
  116.2 0.8 copy-start.7
  131.0 0.7 copy-start.8

commit v2 on v1

v2 whole, which is shorter than its diff:
```python
import functools
import jax
import jax.numpy as jnp
from jax import lax
from jax.experimental import pallas as pl
from jax.experimental.pallas import tpu as pltpu
from jax.sharding import PartitionSpec as P


LANES = 128
SUBS = 8
MICRO = 32
DEPTH = 512
CUTS = (1, 3, 5)
FULL = lax.Precision.HIGHEST


def dot_tn(a, b):
    return lax.dot_general(a, b, (((0,), (0,)), ((), ())), precision=FULL, preferred_element_type=jnp.float32)


def dot_nn(a, b):
    return lax.dot_general(a, b, (((1,), (0,)), ((), ())), precision=FULL, preferred_element_type=jnp.float32)


def row_of(x, i):
    return jnp.broadcast_to(x[i:i + 1, :], x.shape)


def lane_of(x, j):
    return jnp.broadcast_to(x[:, j:j + 1], x.shape)


def eliminate(tiles, first):
    sub = lax.broadcasted_iota(jnp.int32, (SUBS, LANES), 0)
    groups = len(tiles)
    for p in range(groups):
        cols = [[lane_of(tiles[g][0], first + SUBS * p + j) for g in range(p, groups)] for j in range(SUBS)]
        scale = None
        for i in range(SUBS):
            pivot = row_of(cols[i][0], i)
            inv = 1.0 / pivot
            root = lax.rsqrt(pivot)
            scale = root if scale is None else jnp.where(sub == i, root, scale)
            mult = [c * inv for c in cols[i]]
            mult[0] = jnp.where(sub > i, mult[0], 0.0)
            for j in range(i + 1, SUBS):
                e = row_of(cols[j][0], i)
                cols[j] = [c - m * e for c, m in zip(cols[j], mult)]
            for t in range(len(tiles[p])):
                e = row_of(tiles[p][t], i)
                for g in range(p, groups):
                    tiles[g][t] = tiles[g][t] - mult[g - p] * e
        tiles[p] = [t * scale for t in tiles[p]]
    return tiles


def factor_diag(d_ref):
    n = d_ref.shape[0]
    for r0 in range(0, n, MICRO):
        tiles = [[d_ref[r0 + SUBS * g:r0 + SUBS * (g + 1), LANES * t:LANES * (t + 1)] for t in range(2)] for g in range(MICRO // SUBS)]
        tiles = eliminate(tiles, r0)
        for g, row in enumerate(tiles):
            for t, tile in enumerate(row):
                d_ref[r0 + SUBS * g:r0 + SUBS * (g + 1), LANES * t:LANES * (t + 1)] = tile
        r1 = r0 + MICRO
        if r1 < n:
            u = d_ref[r0:r1, :]
            d_ref[r1:, :] = d_ref[r1:, :] - dot_tn(u[:, :LANES], u)[r1:]


def groups_of(size):
    edges = [0, *[c for c in CUTS if c * LANES < size], size // LANES]
    return list(zip(edges[:-1], edges[1:]))


def panels(group, size):
    at, out = 0, []
    for r in range(*group):
        width = size - r * LANES
        out.append((r, at, width))
        at += width
    return out, at


def gram_kernel(groups, count_ref, h_ref, prior_ref, *out_refs):
    k = pl.program_id(0)
    depth, size = h_ref.shape
    left = count_ref[0] - k * depth

    @pl.when(k == 0)
    def _():
        r = lax.broadcasted_iota(jnp.int32, (LANES, LANES), 0)
        c = lax.broadcasted_iota(jnp.int32, (LANES, LANES), 1)
        for group, out_ref in zip(groups, out_refs):
            out_ref[...] = jnp.zeros_like(out_ref)
            for b, at, _ in panels(group, size)[0]:
                diag = jnp.broadcast_to(prior_ref[:, b * LANES:(b + 1) * LANES], (LANES, LANES))
                out_ref[:, at:at + LANES] = jnp.where(r == c, diag, 0.0)

    @pl.when(left > 0)
    def _():
        index = lax.broadcasted_iota(jnp.int32, h_ref.shape, 0)
        h = jnp.where(index < left, h_ref[...], jnp.zeros_like(h_ref))
        for group, out_ref in zip(groups, out_refs):
            first, last = group[0] * LANES, group[1] * LANES
            gram = lax.dot_general(h[:, first:last], h[:, first:], (((0,), (0,)), ((), ())), preferred_element_type=jnp.float32)
            for b, at, width in panels(group, size)[0]:
                r = b * LANES - first
                out_ref[:, at:at + width] += gram[r:r + LANES, r:]


def gram_rows(groups, observations, counts, prior):
    capacity, size = observations.shape
    depth = min(DEPTH, capacity)
    totals = [panels(group, size)[1] for group in groups]

    def block(k, count):
        return jnp.minimum(k, (count[0] - 1) // depth), 0

    grid_spec = pltpu.PrefetchScalarGridSpec(
        num_scalar_prefetch=1,
        grid=(capacity // depth,),
        in_specs=[pl.BlockSpec((depth, size), block), pl.BlockSpec((1, size), lambda k, count: (0, 0))],
        out_specs=[pl.BlockSpec((LANES, total), lambda k, count: (0, 0)) for total in totals],
    )
    return pl.pallas_call(
        functools.partial(gram_kernel, groups),
        out_shape=[jax.ShapeDtypeStruct((LANES, total), jnp.float32) for total in totals],
        grid_spec=grid_spec,
    )(counts, observations, prior)


def factor_kernel(group, odd_ref, own_ref, pair_ref, far_ref, near_ref, *refs):
    start = group[0] * LANES
    if start:
        prev_ref, out_ref, d_ref, o_ref, u_ref, sem = refs
    else:
        out_ref, d_ref, o_ref, sem = refs
    rows, size = o_ref.shape
    if start:
        fetch = pltpu.make_async_copy(prev_ref.at[pl.ds(0, start), pl.ds(start, size - start)], u_ref, sem.at[0])
        fetch.start()
    odd = odd_ref[0] > 0
    total = own_ref[...] + far_ref[...] + near_ref[...] + jnp.where(odd, pair_ref[...], 0.0)
    o_ref[...] = jnp.zeros_like(o_ref)
    r = lax.broadcasted_iota(jnp.int32, (LANES, LANES), 0)
    c = lax.broadcasted_iota(jnp.int32, (LANES, LANES), 1)
    eye = jnp.where(r == c, 1.0, 0.0).astype(jnp.float32)
    if start:
        fetch.wait()
    for b, at, width in panels(group, size)[0]:
        a = total[:, at:at + width]
        s = b * LANES
        if start:
            u = u_ref[:, s - start:]
            a = a - dot_tn(u[:, :LANES], u)
        if s > start:
            u = o_ref[:s - start, s:]
            a = a - dot_tn(u[:, :LANES], u)
        d_ref[:, :LANES] = a[:, :LANES]
        d_ref[:, LANES:] = eye
        factor_diag(d_ref)
        o_ref[s - start:s - start + LANES, s:s + LANES] = jnp.where(r <= c, d_ref[:, :LANES], 0.0)
        if width > LANES:
            o_ref[s - start:s - start + LANES, s + LANES:] = dot_nn(d_ref[:, LANES:], a[:, LANES:])
    put = pltpu.make_async_copy(o_ref, out_ref.at[pl.ds(start, rows), :], sem.at[1])
    put.start()
    put.wait()


def factor_rows(group, size, odd, parts, prev):
    start, rows = group[0] * LANES, (group[1] - group[0]) * LANES
    f32 = jnp.float32
    scratch = [pltpu.VMEM((LANES, 2 * LANES), f32), pltpu.VMEM((rows, size), f32)]
    in_specs = [pl.BlockSpec(memory_space=pltpu.SMEM)] + [pl.BlockSpec(memory_space=pltpu.VMEM)] * len(parts)
    args = [odd, *parts]
    aliases = {}
    if start:
        aliases = {len(args): 0}
        in_specs.append(pl.BlockSpec(memory_space=pl.ANY))
        args.append(prev)
        scratch.append(pltpu.VMEM((start, size - start), f32))
    scratch.append(pltpu.SemaphoreType.DMA((2,)))
    return pl.pallas_call(
        functools.partial(factor_kernel, group),
        out_shape=jax.ShapeDtypeStruct((size, size), f32),
        in_specs=in_specs,
        out_specs=pl.BlockSpec(memory_space=pl.ANY),
        scratch_shapes=scratch,
        input_output_aliases=aliases,
    )(*args)


def body(observations, counts, prior):
    size = observations.shape[1]
    steps = lax.axis_size("tm")
    groups = groups_of(size)
    odd = lax.rem(lax.axis_index("tm"), 2)
    swap = [(t, t ^ 1) for t in range(steps)]
    ahead = [(t, t + 3) for t in range(steps - 3)]
    inward = [(t, t - 1) for t in range(1, steps, 2)]
    owns = []
    for share in (groups[:1], groups[1:2], groups[2:]):
        owns += gram_rows(share, observations, counts, prior)
    parts = []
    for own in owns:
        pair = lax.ppermute(own, "tm", swap)
        send = jnp.where(odd == 0, own + pair, own)
        far = lax.ppermute(send, "tm", ahead)
        near = lax.ppermute(far, "tm", inward)
        parts.append([own, pair, far, near])
    factor = None
    for group, part in zip(groups, parts):
        factor = factor_rows(group, size, odd[None], part, factor)
    return factor[None]


def solution(mesh):
    placed = (P(("grp", "tm"), None), P(("grp", "tm")), P(("grp", "tm"), None))
    return jax.shard_map(
        body, mesh=mesh, in_specs=placed, out_specs=P(("grp", "tm"), None, None), check_vma=False
    )
```

time: 146 us -> 128 us (0.88)
  the two profiles are of different devices: /device:TPU:0 before, /device:TPU:29 now
where the time goes in v2:
time: 128 us; the launch traced here: 127 us
  Pallas kernels  62.5 us (49%)
  starting transfers between devices  50.8 us (40%)
  waiting for transfers between devices  6.3 us (5%)
  local copies, waits for them, and re-layouts  4.04 us (3%)
  other arithmetic  2.39 us (2%)
    pallas_call x4, Pallas kernels, factor_rows(): pl.pallas_call(functools.partial(factor_kernel, group), out_shape=jax.Sha...  54.2 us
    ppermute x4, starting transfers between devices, body(): near = lax.ppermute(far, 'tm', inward)  44.3 us
    pallas_call x3, Pallas kernels, gram_rows(): pl.pallas_call(functools.partial(gram_kernel, groups), out_shape=[jax.Sha...  8.32 us
    ppermute x4, waiting for transfers between devices, body(): far = lax.ppermute(send, 'tm', ahead)  5.95 us
    ppermute x4, starting transfers between devices, body(): far = lax.ppermute(send, 'tm', ahead)  5.14 us
    unnamed x24, local copies, waits for them, and re-layouts  4.04 us
  transfers between devices with their start and end apart: 12, of which 2 were waited for; matrix products, arithmetic and copies ran while one was open for 2% of the time, Pallas kernels for 32%

profile of v2, /device:TPU:29, one launch (start us, length us, event | category | flops | bytes accessed | tf_op | source)
XLA Modules:
  0.0 127.1 jit_solution(17531003732709321196)
XLA Ops:
  0.7 2.8 %shard_map.38.own_ref = f32[128,1664]{1,0:T(8,128)} custom-call(s32[1]{0:T(128)S(6)} %copy.10.count_ref, bf16[2048,1024]{1,0:T(8,128)(2,1)} %h_ref.5, f32[1,1024]{1,0:T(1,128)} %prior_ref.5), custom_call_target="tpu_custom_call" | custom-call | tf_op jit(solution)/shard_map/pallas_call | solution.py:127
  3.5 0.7 collective-permute-start.6
  4.1 3.0 %shard_map.37 = (f32[128,1152]{1,0:T(8,128)}, f32[128,768]{1,0:T(8,128)}) custom-call(s32[1]{0:T(128)S(6)} %copy.10.count_ref, bf16[2048,1024]{1,0:T(8,128)(2,1)} %h_ref.5, f32[1,1024]{1,0:T(1,128)} %prior_ref.5), custom_call_target="tpu_custom_call" | custom-call | tf_op jit(solution)/shard_map/pallas_call | solution.py:127
  7.2 1.0 add_select_fusion
  8.2 1.3 %collective-permute-start.7 = (f32[128,1664]{1,0:T(8,128)}, f32[128,1664]{1,0:T(8,128)}, u32[]{:S(2)}, u32[]{:S(2)}) collective-permute-start(f32[128,1664]{1,0:T(8,128)} %add_select_fusion), channel_id=1, source_target_pairs={{0,3},{1,4},{2,5},{3,6},{4,7},{5,8},{6,9},{7,10},{8,11},{9,12},{10... | collective-permute-start | bytes 2555912 | tf_op jit(solution)/shard_map/ppermute | solution.py:210
  9.5 2.5 %shard_map.39.own_ref = f32[128,1024]{1,0:T(8,128)} custom-call(s32[1]{0:T(128)S(6)} %copy.10.count_ref, bf16[2048,1024]{1,0:T(8,128)(2,1)} %h_ref.5, f32[1,1024]{1,0:T(1,128)} %prior_ref.5), custom_call_target="tpu_custom_call" | custom-call | tf_op jit(solution)/shard_map/pallas_call | solution.py:127
  12.6 1.3 %collective-permute-start.4 = (f32[128,1152]{1,0:T(8,128)S(1)}, f32[128,1152]{1,0:T(8,128)S(1)}, u32[]{:S(2)}, u32[]{:S(2)}) collective-permute-start(f32[128,1152]{1,0:T(8,128)S(1)} %add_select_fusion.1), channel_id=1, source_target_pairs={{0,3},{1,4},{2,5},{3,6},{4,7},{5,8},{6,9},{7,10},{8,11},{9,12},{10... | collective-permute-start | bytes 1769480 | tf_op jit(solution)/shard_map/ppermute | solution.py:210
  14.3 1.3 %add_select_fusion.2 = f32[128,1024]{1,0:T(8,128)S(1)} fusion(f32[128,1024]{1,0:T(8,128)} %shard_map.39.own_ref, f32[128,1024]{1,0:T(8,128)S(1)} %collective-permute-done.9.pair_ref, pred[]{:T(512)S(6)} %eq.2), kind=kLoop, calls=%fused_computation.2 | loop fusion | flops 262144 | bytes 1572865 | tf_op jit(solution)/shard_map/jit(_where)/select_n | solution.py:209
  15.6 1.3 %collective-permute-start.10 = (f32[128,1024]{1,0:T(8,128)S(1)}, f32[128,1024]{1,0:T(8,128)S(1)}, u32[]{:S(2)}, u32[]{:S(2)}) collective-permute-start(f32[128,1024]{1,0:T(8,128)S(1)} %add_select_fusion.2), channel_id=1, source_target_pairs={{0,3},{1,4},{2,5},{3,6},{4,7},{5,8},{6,9},{7,10},{8,11},{9,12},{10... | collective-permute-start | bytes 1572872 | tf_op jit(solution)/shard_map/ppermute | solution.py:210
  16.9 5.9 %collective-permute-done.7.far_ref = f32[128,1664]{1,0:T(8,128)} collective-permute-done((f32[128,1664]{1,0:T(8,128)}, f32[128,1664]{1,0:T(8,128)}, u32[]{:S(2)}, u32[]{:S(2)}) %collective-permute-start.7) | collective-permute-done | bytes 852000 | tf_op jit(solution)/shard_map/ppermute | solution.py:210
  22.8 14.2 %collective-permute-start.8 = (f32[128,1664]{1,0:T(8,128)}, f32[128,1664]{1,0:T(8,128)S(1)}, u32[]{:S(2)}, u32[]{:S(2)}) collective-permute-start(f32[128,1664]{1,0:T(8,128)} %collective-permute-done.7.far_ref), channel_id=1, source_target_pairs={{1,0},{3,2},{5,4},{7,6},{9,8},{11,10},{13,12},{15,14},{17,16},{19,... | collective-permute-start | bytes 2555912 | tf_op jit(solution)/shard_map/ppermute | solution.py:211
  37.1 0.7 copy-done.6
  37.8 1.3 %collective-permute-start.1 = (f32[128,768]{1,0:T(8,128)S(1)}, f32[128,768]{1,0:T(8,128)}, u32[]{:S(2)}, u32[]{:S(2)}) collective-permute-start(f32[128,768]{1,0:T(8,128)S(1)} %add_select_fusion.3), channel_id=1, source_target_pairs={{0,3},{1,4},{2,5},{3,6},{4,7},{5,8},{6,9},{7,10},{8,11},{9,12},{10... | collective-permute-start | bytes 1179656 | tf_op jit(solution)/shard_map/ppermute | solution.py:210
  39.1 10.4 %collective-permute-start.5 = (f32[128,1152]{1,0:T(8,128)S(1)}, f32[128,1152]{1,0:T(8,128)S(1)}, u32[]{:S(2)}, u32[]{:S(2)}) collective-permute-start(f32[128,1152]{1,0:T(8,128)S(1)} %collective-permute-done.4.far_ref), channel_id=1, source_target_pairs={{1,0},{3,2},{5,4},{7,6},{9,8},{11,10},{13,12},{15,14},{17,16},{19,... | collective-permute-start | bytes 1769480 | tf_op jit(solution)/shard_map/ppermute | solution.py:211
  49.6 0.8 copy-done.10
  50.4 11.2 %collective-permute-start.11 = (f32[128,1024]{1,0:T(8,128)S(1)}, f32[128,1024]{1,0:T(8,128)S(1)}, u32[]{:S(2)}, u32[]{:S(2)}) collective-permute-start(f32[128,1024]{1,0:T(8,128)S(1)} %collective-permute-done.10.far_ref), channel_id=1, source_target_pairs={{1,0},{3,2},{5,4},{7,6},{9,8},{11,10},{13,12},{15,14},{17,16},{19,... | collective-permute-start | bytes 1572872 | tf_op jit(solution)/shard_map/ppermute | solution.py:211
  61.6 8.5 %collective-permute-start.2 = (f32[128,768]{1,0:T(8,128)}, f32[128,768]{1,0:T(8,128)}, u32[]{:S(2)}, u32[]{:S(2)}) collective-permute-start(f32[128,768]{1,0:T(8,128)} %collective-permute-done.1.far_ref), channel_id=1, source_target_pairs={{1,0},{3,2},{5,4},{7,6},{9,8},{11,10},{13,12},{15,14},{17,16},{19,... | collective-permute-start | bytes 1179656 | tf_op jit(solution)/shard_map/ppermute | solution.py:211
  70.1 0.8 copy-done.11
  70.9 7.1 %shard_map.40.refs_0_ = f32[1024,1024]{1,0:T(8,128)} custom-call(s32[1]{0:T(128)} %bitcast.odd_ref, f32[128,1024]{1,0:T(8,128)} %shard_map.39.own_ref, f32[128,1024]{1,0:T(8,128)} %copy-done.4, f32[128,1024]{1,0:T(8,128)} %copy-done.10, f32[128,1024]{1,0:T(8,128)} %copy-done.11), custom_call_target="tpu_custom_call" | custom-call | tf_op jit(solution)/shard_map/pallas_call | solution.py:185
  78.0 0.9 copy-done.7
  78.9 14.2 %shard_map.41.refs_0_ = f32[1024,1024]{1,0:T(8,128)} custom-call(s32[1]{0:T(128)} %bitcast.odd_ref, f32[128,1664]{1,0:T(8,128)} %shard_map.38.own_ref, f32[128,1664]{1,0:T(8,128)} %copy-done.1, f32[128,1664]{1,0:T(8,128)} %collective-permute-done.7.far_ref, f32[128,1664]{1,0:T(8,128)} %copy-done.7, ...), custom_call_target="tpu_custom_call", output_to_operand_aliasing={{}: (5, {})} | custom-call | tf_op jit(solution)/shard_map/pallas_call | solution.py:185
  93.2 0.8 copy-done.9
  94.0 14.4 %shard_map.42.refs_0_ = f32[1024,1024]{1,0:T(8,128)} custom-call(s32[1]{0:T(128)} %bitcast.odd_ref, f32[128,1152]{1,0:T(8,128)} %get-tuple-element.8.own_ref, f32[128,1152]{1,0:T(8,128)} %copy-done.3, f32[128,1152]{1,0:T(8,128)} %copy-done.8, f32[128,1152]{1,0:T(8,128)} %copy-done.9, f32[1024,1024]{1,0:T(8,128)} %shard_map.41.refs_0_), custom_call_target="tpu_custom_call", output_to_operand_aliasing={{}: (5, {})} | custom-call | tf_op jit(solution)/shard_map/pallas_call | solution.py:185
  108.4 18.5 %shard_map.43 = f32[1024,1024]{1,0:T(8,128)} custom-call(s32[1]{0:T(128)} %bitcast.odd_ref, f32[128,768]{1,0:T(8,128)} %get-tuple-element.7.own_ref, f32[128,768]{1,0:T(8,128)} %copy-done.6, f32[128,768]{1,0:T(8,128)} %collective-permute-done.1.far_ref, f32[128,768]{1,0:T(8,128)} %collective-permute-done.2.near_ref, ...), custom_call_target="tpu_custom_call", output_to_operand_aliasing={{}: (5, {})} | custom-call | tf_op jit(solution)/shard_map/pallas_call | solution.py:185
  (35 shorter events, 1.1 us)
Async XLA Ops:
  3.4 3.8 %copy-start = (f32[128,1664]{1,0:T(8,128)S(1)}, f32[128,1664]{1,0:T(8,128)}, u32[]{:S(2)}) copy-start(f32[128,1664]{1,0:T(8,128)} %shard_map.38.own_ref) | copy-start | bytes 2555908
  3.5 3.8 %collective-permute-start.6 = (f32[128,1664]{1,0:T(8,128)}, f32[128,1664]{1,0:T(8,128)S(1)}, u32[]{:S(2)}, u32[]{:S(2)}) collective-permute-start(f32[128,1664]{1,0:T(8,128)} %shard_map.38.own_ref), channel_id=1, source_target_pairs={{0,1},{1,0},{2,3},{3,2},{4,5},{5,4},{6,7},{7,6},{8,9},{9,8},{10,11... | collective-permute-start | bytes 2555912 | tf_op jit(solution)/shard_map/ppermute | solution.py:208
  7.1 5.4 %copy-start.5 = (f32[128,768]{1,0:T(8,128)S(1)}, f32[128,768]{1,0:T(8,128)}, u32[]{:S(2)}) copy-start(f32[128,768]{1,0:T(8,128)} %get-tuple-element.7.own_ref) | copy-start | bytes 1179652
  7.1 5.4 %copy-start.2 = (f32[128,1152]{1,0:T(8,128)S(1)}, f32[128,1152]{1,0:T(8,128)}, u32[]{:S(2)}) copy-start(f32[128,1152]{1,0:T(8,128)} %get-tuple-element.8.own_ref) | copy-start | bytes 1769476
  7.1 5.4 %collective-permute-start.3 = (f32[128,1152]{1,0:T(8,128)}, f32[128,1152]{1,0:T(8,128)S(1)}, u32[]{:S(2)}, u32[]{:S(2)}) collective-permute-start(f32[128,1152]{1,0:T(8,128)} %get-tuple-element.8.own_ref), channel_id=1, source_target_pairs={{0,1},{1,0},{2,3},{3,2},{4,5},{5,4},{6,7},{7,6},{8,9},{9,8},{10,11... | collective-permute-start | bytes 1769480 | tf_op jit(solution)/shard_map/ppermute | solution.py:208
  7.2 5.4 %copy-start.1 = (f32[128,1664]{1,0:T(8,128)}, f32[128,1664]{1,0:T(8,128)S(1)}, u32[]{:S(2)}) copy-start(f32[128,1664]{1,0:T(8,128)S(1)} %collective-permute-done.6.pair_ref) | copy-start | bytes 2555908
  8.2 14.6 %collective-permute-start.7 = (f32[128,1664]{1,0:T(8,128)}, f32[128,1664]{1,0:T(8,128)}, u32[]{:S(2)}, u32[]{:S(2)}) collective-permute-start(f32[128,1664]{1,0:T(8,128)} %add_select_fusion), channel_id=1, source_target_pairs={{0,3},{1,4},{2,5},{3,6},{4,7},{5,8},{6,9},{7,10},{8,11},{9,12},{10... | collective-permute-start | bytes 2555912 | tf_op jit(solution)/shard_map/ppermute | solution.py:210
  12.0 2.3 %collective-permute-start.9 = (f32[128,1024]{1,0:T(8,128)}, f32[128,1024]{1,0:T(8,128)S(1)}, u32[]{:S(2)}, u32[]{:S(2)}) collective-permute-start(f32[128,1024]{1,0:T(8,128)} %shard_map.39.own_ref), channel_id=1, source_target_pairs={{0,1},{1,0},{2,3},{3,2},{4,5},{5,4},{6,7},{7,6},{8,9},{9,8},{10,11... | collective-permute-start | bytes 1572872 | tf_op jit(solution)/shard_map/ppermute | solution.py:208
  12.5 24.5 %collective-permute-start = (f32[128,768]{1,0:T(8,128)S(1)}, f32[128,768]{1,0:T(8,128)S(1)}, u32[]{:S(2)}, u32[]{:S(2)}) collective-permute-start(f32[128,768]{1,0:T(8,128)S(1)} %copy-done.5), channel_id=1, source_target_pairs={{0,1},{1,0},{2,3},{3,2},{4,5},{5,4},{6,7},{7,6},{8,9},{9,8},{10,11... | collective-permute-start | bytes 1179656 | tf_op jit(solution)/shard_map/ppermute | solution.py:208
  12.6 65.4 %copy-start.3 = (f32[128,1152]{1,0:T(8,128)}, f32[128,1152]{1,0:T(8,128)S(1)}, u32[]{:S(2)}) copy-start(f32[128,1152]{1,0:T(8,128)S(1)} %collective-permute-done.3.pair_ref) | copy-start | bytes 1769476
  12.6 26.5 %collective-permute-start.4 = (f32[128,1152]{1,0:T(8,128)S(1)}, f32[128,1152]{1,0:T(8,128)S(1)}, u32[]{:S(2)}, u32[]{:S(2)}) collective-permute-start(f32[128,1152]{1,0:T(8,128)S(1)} %add_select_fusion.1), channel_id=1, source_target_pairs={{0,3},{1,4},{2,5},{3,6},{4,7},{5,8},{6,9},{7,10},{8,11},{9,12},{10... | collective-permute-start | bytes 1769480 | tf_op jit(solution)/shard_map/ppermute | solution.py:210
  14.3 56.6 %copy-start.4 = (f32[128,1024]{1,0:T(8,128)}, f32[128,1024]{1,0:T(8,128)S(1)}, u32[]{:S(2)}) copy-start(f32[128,1024]{1,0:T(8,128)S(1)} %collective-permute-done.9.pair_ref) | copy-start | bytes 1572868
  15.6 34.0 %collective-permute-start.10 = (f32[128,1024]{1,0:T(8,128)S(1)}, f32[128,1024]{1,0:T(8,128)S(1)}, u32[]{:S(2)}, u32[]{:S(2)}) collective-permute-start(f32[128,1024]{1,0:T(8,128)S(1)} %add_select_fusion.2), channel_id=1, source_target_pairs={{0,3},{1,4},{2,5},{3,6},{4,7},{5,8},{6,9},{7,10},{8,11},{9,12},{10... | collective-permute-start | bytes 1572872 | tf_op jit(solution)/shard_map/ppermute | solution.py:210
  22.8 55.2 %collective-permute-start.8 = (f32[128,1664]{1,0:T(8,128)}, f32[128,1664]{1,0:T(8,128)S(1)}, u32[]{:S(2)}, u32[]{:S(2)}) collective-permute-start(f32[128,1664]{1,0:T(8,128)} %collective-permute-done.7.far_ref), channel_id=1, source_target_pairs={{1,0},{3,2},{5,4},{7,6},{9,8},{11,10},{13,12},{15,14},{17,16},{19,... | collective-permute-start | bytes 2555912 | tf_op jit(solution)/shard_map/ppermute | solution.py:211
  37.1 0.8 copy-start.6
  37.8 23.8 %collective-permute-start.1 = (f32[128,768]{1,0:T(8,128)S(1)}, f32[128,768]{1,0:T(8,128)}, u32[]{:S(2)}, u32[]{:S(2)}) collective-permute-start(f32[128,768]{1,0:T(8,128)S(1)} %add_select_fusion.3), channel_id=1, source_target_pairs={{0,3},{1,4},{2,5},{3,6},{4,7},{5,8},{6,9},{7,10},{8,11},{9,12},{10... | collective-permute-start | bytes 1179656 | tf_op jit(solution)/shard_map/ppermute | solution.py:210
  39.1 54.0 %copy-start.8 = (f32[128,1152]{1,0:T(8,128)}, f32[128,1152]{1,0:T(8,128)S(1)}, u32[]{:S(2)}) copy-start(f32[128,1152]{1,0:T(8,128)S(1)} %collective-permute-done.4.far_ref) | copy-start | bytes 1769476
  39.1 54.0 %collective-permute-start.5 = (f32[128,1152]{1,0:T(8,128)S(1)}, f32[128,1152]{1,0:T(8,128)S(1)}, u32[]{:S(2)}, u32[]{:S(2)}) collective-permute-start(f32[128,1152]{1,0:T(8,128)S(1)} %collective-permute-done.4.far_ref), channel_id=1, source_target_pairs={{1,0},{3,2},{5,4},{7,6},{9,8},{11,10},{13,12},{15,14},{17,16},{19,... | collective-permute-start | bytes 1769480 | tf_op jit(solution)/shard_map/ppermute | solution.py:211
  49.6 0.8 copy-start.10
  50.4 19.7 %collective-permute-start.11 = (f32[128,1024]{1,0:T(8,128)S(1)}, f32[128,1024]{1,0:T(8,128)S(1)}, u32[]{:S(2)}, u32[]{:S(2)}) collective-permute-start(f32[128,1024]{1,0:T(8,128)S(1)} %collective-permute-done.10.far_ref), channel_id=1, source_target_pairs={{1,0},{3,2},{5,4},{7,6},{9,8},{11,10},{13,12},{15,14},{17,16},{19,... | collective-permute-start | bytes 1572872 | tf_op jit(solution)/shard_map/ppermute | solution.py:211
  61.6 46.8 %collective-permute-start.2 = (f32[128,768]{1,0:T(8,128)}, f32[128,768]{1,0:T(8,128)}, u32[]{:S(2)}, u32[]{:S(2)}) collective-permute-start(f32[128,768]{1,0:T(8,128)} %collective-permute-done.1.far_ref), channel_id=1, source_target_pairs={{1,0},{3,2},{5,4},{7,6},{9,8},{11,10},{13,12},{15,14},{17,16},{19,... | collective-permute-start | bytes 1179656 | tf_op jit(solution)/shard_map/ppermute | solution.py:211
  70.1 0.8 copy-start.11
  78.0 0.9 copy-start.7
  93.2 0.8 copy-start.9

commit v3 on v2

--- a/solution.py
+++ b/solution.py
@@ -11,16 +11,32 @@
 SUBS = 8
 MICRO = 32
 DEPTH = 512
-CUTS = (1, 3, 5)
-FULL = lax.Precision.HIGHEST
-
-
-def dot_tn(a, b):
-    return lax.dot_general(a, b, (((0,), (0,)), ((), ())), precision=FULL, preferred_element_type=jnp.float32)
-
-
-def dot_nn(a, b):
-    return lax.dot_general(a, b, (((1,), (0,)), ((), ())), precision=FULL, preferred_element_type=jnp.float32)
+ROOM = 24 << 20
+CUTS = (1, 2, 4)
+
+
+def parts_of(x):
+    out = []
+    for _ in range(3):
+        out.append(x.astype(jnp.bfloat16))
+        x = x - out[-1].astype(jnp.float32)
+    return out
+
+
+def exact_tn(a, b):
+    a, b = parts_of(a), parts_of(b)
+    order = ((0, 0), (0, 1), (1, 0), (1, 1), (0, 2), (2, 0))
+    left = jnp.concatenate([a[i] for i, _ in order], 0)
+    right = jnp.concatenate([b[j] for _, j in order], 0)
+    return lax.dot_general(left, right, (((0,), (0,)), ((), ())), preferred_element_type=jnp.float32)
+
+
+def exact_nn(a, b):
+    a, b = parts_of(a), parts_of(b)
+    order = ((0, 0), (0, 1), (1, 0), (1, 1), (0, 2), (2, 0))
+    left = jnp.concatenate([a[i] for i, _ in order], 1)
+    right = jnp.concatenate([b[j] for _, j in order], 0)
+    return lax.dot_general(left, right, (((1,), (0,)), ((), ())), preferred_element_type=jnp.float32)
 
 
 def row_of(x, i):
@@ -28,7 +44,7 @@
 
 
 def lane_of(x, j):
-    return jnp.broadcast_to(x[:, j:j + 1], x.shape)
+    return jnp.take_along_axis(x, jnp.full(x.shape, j, jnp.int32), axis=1)
 
 
 def eliminate(tiles, first):
@@ -36,22 +52,37 @@
     groups = len(tiles)
     for p in range(groups):
         cols = [[lane_of(tiles[g][0], first + SUBS * p + j) for g in range(p, groups)] for j in range(SUBS)]
-        scale = None
-        for i in range(SUBS):
-            pivot = row_of(cols[i][0], i)
-            inv = 1.0 / pivot
-            root = lax.rsqrt(pivot)
-            scale = root if scale is None else jnp.where(sub == i, root, scale)
-            mult = [c * inv for c in cols[i]]
-            mult[0] = jnp.where(sub > i, mult[0], 0.0)
-            for j in range(i + 1, SUBS):
-                e = row_of(cols[j][0], i)
-                cols[j] = [c - m * e for c, m in zip(cols[j], mult)]
+        scale, mix = None, None
+        for i in range(0, SUBS, 2):
+            x, y = cols[i], cols[i + 1]
+            aa, ab, bb = row_of(x[0], i), row_of(y[0], i), row_of(y[0], i + 1)
+            det = aa * bb - ab * ab
+            ra, rd = 1.0 / aa, 1.0 / det
+            root = lax.rsqrt(aa)
+            tail = aa * root * lax.rsqrt(det)
+            skew = ab * ra
+            scale = jnp.where(sub == i + 1, tail, root if scale is None else jnp.where(sub == i, root, scale))
+            mix = jnp.where(sub == i + 1, skew, 0.0 if mix is None else mix)
+            w = [v * aa - u * ab for u, v in zip(x, y)]
+            x = [jnp.where(sub > i + 1, x[0], 0.0), *x[1:]]
+            w[0] = jnp.where(sub > i + 1, w[0], 0.0)
+            mx, mw = [v * ra for v in x], [v * rd for v in w]
+            for j in range(i + 2, SUBS):
+                e, f = row_of(cols[j][0], i), row_of(cols[j][0], i + 1)
+                h = f * aa - e * ab
+                if j < i + 4:
+                    cols[j] = [(c - (u * e) * ra) - ((v * h) * ra) * rd for c, u, v in zip(cols[j], x, w)]
+                else:
+                    h = h * ra
+                    cols[j] = [c - u * e - v * h for c, u, v in zip(cols[j], mx, mw)]
             for t in range(len(tiles[p])):
-                e = row_of(tiles[p][t], i)
+                e, f = row_of(tiles[p][t], i), row_of(tiles[p][t], i + 1)
+                h = f - skew * e
                 for g in range(p, groups):
-                    tiles[g][t] = tiles[g][t] - mult[g - p] * e
-        tiles[p] = [t * scale for t in tiles[p]]
+                    tiles[g][t] = tiles[g][t] - mx[g - p] * e - mw[g - p] * h
+        for t in range(len(tiles[p])):
+            v = tiles[p][t]
+            tiles[p][t] = (v - mix * pltpu.roll(v, 1, 0)) * scale
     return tiles
 
 
@@ -66,7 +97,7 @@
         r1 = r0 + MICRO
         if r1 < n:
             u = d_ref[r0:r1, :]
-            d_ref[r1:, :] = d_ref[r1:, :] - dot_tn(u[:, :LANES], u)[r1:]
+            d_ref[r1:, :] = d_ref[r1:, :] - exact_tn(u[:, :LANES], u)[r1:]
 
 
 def groups_of(size):
@@ -98,16 +129,22 @@
                 diag = jnp.broadcast_to(prior_ref[:, b * LANES:(b + 1) * LANES], (LANES, LANES))
                 out_ref[:, at:at + LANES] = jnp.where(r == c, diag, 0.0)
 
-    @pl.when(left > 0)
-    def _():
-        index = lax.broadcasted_iota(jnp.int32, h_ref.shape, 0)
-        h = jnp.where(index < left, h_ref[...], jnp.zeros_like(h_ref))
+    def add(h):
         for group, out_ref in zip(groups, out_refs):
             first, last = group[0] * LANES, group[1] * LANES
             gram = lax.dot_general(h[:, first:last], h[:, first:], (((0,), (0,)), ((), ())), preferred_element_type=jnp.float32)
             for b, at, width in panels(group, size)[0]:
                 r = b * LANES - first
                 out_ref[:, at:at + width] += gram[r:r + LANES, r:]
+
+    @pl.when(left >= depth)
+    def _():
+        add(h_ref[...])
+
+    @pl.when(jnp.logical_and(left > 0, left < depth))
+    def _():
+        index = lax.broadcasted_iota(jnp.int32, h_ref.shape, 0)
+        add(jnp.where(index < left, h_ref[...], jnp.zeros_like(h_ref)))
 
 
 def gram_rows(groups, observations, counts, prior):
@@ -128,6 +165,7 @@
         functools.partial(gram_kernel, groups),
         out_shape=[jax.ShapeDtypeStruct((LANES, total), jnp.float32) for total in totals],
         grid_spec=grid_spec,
+        compiler_params=pltpu.CompilerParams(vmem_limit_bytes=ROOM),
     )(counts, observations, prior)
 
 
@@ -154,16 +192,16 @@
         s = b * LANES
         if start:
             u = u_ref[:, s - start:]
-            a = a - dot_tn(u[:, :LANES], u)
+            a = a - exact_tn(u[:, :LANES], u)
         if s > start:
             u = o_ref[:s - start, s:]
-            a = a - dot_tn(u[:, :LANES], u)
+            a = a - exact_tn(u[:, :LANES], u)
         d_ref[:, :LANES] = a[:, :LANES]
         d_ref[:, LANES:] = eye
         factor_diag(d_ref)
         o_ref[s - start:s - start + LANES, s:s + LANES] = jnp.where(r <= c, d_ref[:, :LANES], 0.0)
         if width > LANES:
-            o_ref[s - start:s - start + LANES, s + LANES:] = dot_nn(d_ref[:, LANES:], a[:, LANES:])
+            o_ref[s - start:s - start + LANES, s + LANES:] = exact_nn(d_ref[:, LANES:], a[:, LANES:])
     put = pltpu.make_async_copy(o_ref, out_ref.at[pl.ds(start, rows), :], sem.at[1])
     put.start()
     put.wait()
@@ -189,6 +227,7 @@
         out_specs=pl.BlockSpec(memory_space=pl.ANY),
         scratch_shapes=scratch,
         input_output_aliases=aliases,
+        compiler_params=pltpu.CompilerParams(vmem_limit_bytes=ROOM),
     )(*args)
 
 
@@ -201,7 +240,7 @@
     ahead = [(t, t + 3) for t in range(steps - 3)]
     inward = [(t, t - 1) for t in range(1, steps, 2)]
     owns = []
-    for share in (groups[:1], groups[1:2], groups[2:]):
+    for share in (groups[:1], groups[1:]):
         owns += gram_rows(share, observations, counts, prior)
     parts = []
     for own in owns:

time: 128 us -> 103 us (0.80)
  the two profiles are of different devices: /device:TPU:29 before, /device:TPU:21 now
where the time goes in v3:
time: 103 us
  Pallas kernels  40.2 us (39%)
  starting transfers between devices  30.3 us (29%)
  waiting for transfers between devices  25.9 us (25%)
  local copies, waits for them, and re-layouts  2.87 us (3%)
  other arithmetic  2.45 us (2%)
    pallas_call x4, Pallas kernels, factor_rows(): pl.pallas_call(functools.partial(factor_kernel, group), out_shape=jax.Sha...  35.6 us
    ppermute x4, waiting for transfers between devices, body(): far = lax.ppermute(send, 'tm', ahead)  25.9 us
    ppermute x4, starting transfers between devices, body(): near = lax.ppermute(far, 'tm', inward)  20.2 us
    ppermute x4, starting transfers between devices, body(): far = lax.ppermute(send, 'tm', ahead)  7.68 us
    pallas_call x2, Pallas kernels, gram_rows(): pl.pallas_call(functools.partial(gram_kernel, groups), out_shape=[jax.Sha...  4.6 us
    unnamed x4, local copies, waits for them, and re-layouts  2.87 us
    ppermute x4, starting transfers between devices, body(): pair = lax.ppermute(own, 'tm', swap)  2.47 us
    select_n x4, other arithmetic, body(): send = jnp.where(odd == 0, own + pair, own)  2.45 us
  transfers between devices with their start and end apart: 12, of which 4 were waited for; matrix products, arithmetic and copies ran while one was open for 2% of the time, Pallas kernels for 21%

profile of v3, /device:TPU:21, one launch (start us, length us, event | category | flops | bytes accessed | tf_op | source)
XLA Modules:
  0.0 102.7 jit_solution(7105571442806882056)
XLA Ops:
  0.7 2.2 %copy-done = bf16[2048,1024]{1,0:T(8,128)(2,1)S(1)} copy-done((bf16[2048,1024]{1,0:T(8,128)(2,1)S(1)}, bf16[2048,1024]{1,0:T(8,128)(2,1)}, u32[]{:S(2)}) %copy-start) | copy-done | bytes 4194328
  2.8 0.7 copy-done.1
  3.5 3.4 %shard_map.37 = (f32[128,896]{1,0:T(8,128)}, f32[128,1408]{1,0:T(8,128)S(1)}, f32[128,1280]{1,0:T(8,128)S(1)}) custom-call(s32[1]{0:T(128)S(6)} %copy.10.count_ref, bf16[2048,1024]{1,0:T(8,128)(2,1)S(1)} %copy-done, f32[1,1024]{1,0:T(1,128)S(1)} %copy-done.1), custom_call_target="tpu_custom_call" | custom-call | tf_op jit(solution)/shard_map/pallas_call | solution.py:164
  7.0 1.5 %collective-permute-start.3 = (f32[128,1408]{1,0:T(8,128)S(1)}, f32[128,1408]{1,0:T(8,128)S(1)}, u32[]{:S(2)}, u32[]{:S(2)}) collective-permute-start(f32[128,1408]{1,0:T(8,128)S(1)} %get-tuple-element.9.own_ref), channel_id=1, source_target_pairs={{0,1},{1,0},{2,3},{3,2},{4,5},{5,4},{6,7},{7,6},{8,9},{9,8},{10,11... | collective-permute-start | bytes 2162696 | tf_op jit(solution)/shard_map/ppermute | solution.py:247
  8.4 1.2 %shard_map.38.own_ref = f32[128,1024]{1,0:T(8,128)S(1)} custom-call(s32[1]{0:T(128)S(6)} %copy.10.count_ref, bf16[2048,1024]{1,0:T(8,128)(2,1)S(1)} %copy-done, f32[1,1024]{1,0:T(1,128)S(1)} %copy-done.1), custom_call_target="tpu_custom_call" | custom-call | tf_op jit(solution)/shard_map/pallas_call | solution.py:164
  9.6 0.9 collective-permute-start.9
  10.7 1.9 %collective-permute-start.4 = (f32[128,1408]{1,0:T(8,128)S(1)}, f32[128,1408]{1,0:T(8,128)S(1)}, u32[]{:S(2)}, u32[]{:S(2)}) collective-permute-start(f32[128,1408]{1,0:T(8,128)S(1)} %add_select_fusion), channel_id=1, source_target_pairs={{0,3},{1,4},{2,5},{3,6},{4,7},{5,8},{6,9},{7,10},{8,11},{9,12},{10... | collective-permute-start | bytes 2162696 | tf_op jit(solution)/shard_map/ppermute | solution.py:249
  12.7 1.9 %collective-permute-start.1 = (f32[128,1280]{1,0:T(8,128)S(1)}, f32[128,1280]{1,0:T(8,128)S(1)}, u32[]{:S(2)}, u32[]{:S(2)}) collective-permute-start(f32[128,1280]{1,0:T(8,128)S(1)} %add_select_fusion.1), channel_id=1, source_target_pairs={{0,3},{1,4},{2,5},{3,6},{4,7},{5,8},{6,9},{7,10},{8,11},{9,12},{10... | collective-permute-start | bytes 1966088 | tf_op jit(solution)/shard_map/ppermute | solution.py:249
  14.6 1.1 %add_select_fusion.2 = f32[128,1024]{1,0:T(8,128)S(1)} fusion(f32[128,1024]{1,0:T(8,128)S(1)} %shard_map.38.own_ref, f32[128,1024]{1,0:T(8,128)} %collective-permute-done.9.pair_ref, pred[]{:T(512)S(6)} %eq.2), kind=kLoop, calls=%fused_computation.2 | loop fusion | flops 262144 | bytes 1572865 | tf_op jit(solution)/shard_map/jit(_where)/select_n | solution.py:248
  15.8 1.9 %collective-permute-start.10 = (f32[128,1024]{1,0:T(8,128)S(1)}, f32[128,1024]{1,0:T(8,128)S(1)}, u32[]{:S(2)}, u32[]{:S(2)}) collective-permute-start(f32[128,1024]{1,0:T(8,128)S(1)} %add_select_fusion.2), channel_id=1, source_target_pairs={{0,3},{1,4},{2,5},{3,6},{4,7},{5,8},{6,9},{7,10},{8,11},{9,12},{10... | collective-permute-start | bytes 1572872 | tf_op jit(solution)/shard_map/ppermute | solution.py:249
  17.7 1.2 %add_select_fusion.3 = f32[128,896]{1,0:T(8,128)S(1)} fusion(f32[128,896]{1,0:T(8,128)} %get-tuple-element.10.own_ref, f32[128,896]{1,0:T(8,128)} %collective-permute-done.6.pair_ref, pred[]{:T(512)S(6)} %eq.2), kind=kLoop, calls=%fused_computation.3 | loop fusion | flops 229376 | bytes 1376257 | tf_op jit(solution)/shard_map/jit(_where)/select_n | solution.py:248
  18.9 1.9 %collective-permute-start.7 = (f32[128,896]{1,0:T(8,128)S(1)}, f32[128,896]{1,0:T(8,128)S(1)}, u32[]{:S(2)}, u32[]{:S(2)}) collective-permute-start(f32[128,896]{1,0:T(8,128)S(1)} %add_select_fusion.3), channel_id=1, source_target_pairs={{0,3},{1,4},{2,5},{3,6},{4,7},{5,8},{6,9},{7,10},{8,11},{9,12},{10... | collective-permute-start | bytes 1376264 | tf_op jit(solution)/shard_map/ppermute | solution.py:249
  20.8 7.1 %collective-permute-done.4.far_ref = f32[128,1408]{1,0:T(8,128)S(1)} collective-permute-done((f32[128,1408]{1,0:T(8,128)S(1)}, f32[128,1408]{1,0:T(8,128)S(1)}, u32[]{:S(2)}, u32[]{:S(2)}) %collective-permute-start.4) | collective-permute-done | bytes 720928 | tf_op jit(solution)/shard_map/ppermute | solution.py:249
  27.9 5.4 %collective-permute-start.5 = (f32[128,1408]{1,0:T(8,128)S(1)}, f32[128,1408]{1,0:T(8,128)S(1)}, u32[]{:S(2)}, u32[]{:S(2)}) collective-permute-start(f32[128,1408]{1,0:T(8,128)S(1)} %collective-permute-done.4.far_ref), channel_id=1, source_target_pairs={{1,0},{3,2},{5,4},{7,6},{9,8},{11,10},{13,12},{15,14},{17,16},{19,... | collective-permute-start | bytes 2162696 | tf_op jit(solution)/shard_map/ppermute | solution.py:250
  33.4 8.6 %collective-permute-done.1.far_ref = f32[128,1280]{1,0:T(8,128)S(1)} collective-permute-done((f32[128,1280]{1,0:T(8,128)S(1)}, f32[128,1280]{1,0:T(8,128)S(1)}, u32[]{:S(2)}, u32[]{:S(2)}) %collective-permute-start.1) | collective-permute-done | bytes 655392 | tf_op jit(solution)/shard_map/ppermute | solution.py:249
  42.0 5.4 %collective-permute-start.2 = (f32[128,1280]{1,0:T(8,128)S(1)}, f32[128,1280]{1,0:T(8,128)S(1)}, u32[]{:S(2)}, u32[]{:S(2)}) collective-permute-start(f32[128,1280]{1,0:T(8,128)S(1)} %collective-permute-done.1.far_ref), channel_id=1, source_target_pairs={{1,0},{3,2},{5,4},{7,6},{9,8},{11,10},{13,12},{15,14},{17,16},{19,... | collective-permute-start | bytes 1966088 | tf_op jit(solution)/shard_map/ppermute | solution.py:250
  47.4 5.8 %collective-permute-done.10.far_ref = f32[128,1024]{1,0:T(8,128)S(1)} collective-permute-done((f32[128,1024]{1,0:T(8,128)S(1)}, f32[128,1024]{1,0:T(8,128)S(1)}, u32[]{:S(2)}, u32[]{:S(2)}) %collective-permute-start.10) | collective-permute-done | bytes 524320 | tf_op jit(solution)/shard_map/ppermute | solution.py:249
  53.2 5.4 %collective-permute-start.11 = (f32[128,1024]{1,0:T(8,128)S(1)}, f32[128,1024]{1,0:T(8,128)S(1)}, u32[]{:S(2)}, u32[]{:S(2)}) collective-permute-start(f32[128,1024]{1,0:T(8,128)S(1)} %collective-permute-done.10.far_ref), channel_id=1, source_target_pairs={{1,0},{3,2},{5,4},{7,6},{9,8},{11,10},{13,12},{15,14},{17,16},{19,... | collective-permute-start | bytes 1572872 | tf_op jit(solution)/shard_map/ppermute | solution.py:250
  58.7 4.4 %collective-permute-done.7.far_ref = f32[128,896]{1,0:T(8,128)S(1)} collective-permute-done((f32[128,896]{1,0:T(8,128)S(1)}, f32[128,896]{1,0:T(8,128)S(1)}, u32[]{:S(2)}, u32[]{:S(2)}) %collective-permute-start.7) | collective-permute-done | bytes 458784 | tf_op jit(solution)/shard_map/ppermute | solution.py:249
  63.1 3.8 %collective-permute-start.8 = (f32[128,896]{1,0:T(8,128)S(1)}, f32[128,896]{1,0:T(8,128)S(1)}, u32[]{:S(2)}, u32[]{:S(2)}) collective-permute-start(f32[128,896]{1,0:T(8,128)S(1)} %collective-permute-done.7.far_ref), channel_id=1, source_target_pairs={{1,0},{3,2},{5,4},{7,6},{9,8},{11,10},{13,12},{15,14},{17,16},{19,... | collective-permute-start | bytes 1376264 | tf_op jit(solution)/shard_map/ppermute | solution.py:250
  66.9 4.9 %shard_map.39.refs_0_ = f32[1024,1024]{1,0:T(8,128)} custom-call(s32[1]{0:T(128)} %bitcast.odd_ref, f32[128,1024]{1,0:T(8,128)S(1)} %shard_map.38.own_ref, f32[128,1024]{1,0:T(8,128)} %collective-permute-done.9.pair_ref, f32[128,1024]{1,0:T(8,128)S(1)} %collective-permute-done.10.far_ref, f32[128,1024]{1,0:T(8,128)S(1)} %collective-permute-done.11.near_ref), custom_call_target="tpu_custom_call" | custom-call | tf_op jit(solution)/shard_map/pallas_call | solution.py:223
  71.8 6.4 %shard_map.40.refs_0_ = f32[1024,1024]{1,0:T(8,128)} custom-call(s32[1]{0:T(128)} %bitcast.odd_ref, f32[128,896]{1,0:T(8,128)} %get-tuple-element.10.own_ref, f32[128,896]{1,0:T(8,128)} %collective-permute-done.6.pair_ref, f32[128,896]{1,0:T(8,128)S(1)} %collective-permute-done.7.far_ref, ...), custom_call_target="tpu_custom_call", output_to_operand_aliasing={{}: (5, {})} | custom-call | tf_op jit(solution)/shard_map/pallas_call | solution.py:223
  78.3 8.7 %shard_map.41.refs_0_ = f32[1024,1024]{1,0:T(8,128)} custom-call(s32[1]{0:T(128)} %bitcast.odd_ref, f32[128,1408]{1,0:T(8,128)S(1)} %get-tuple-element.9.own_ref, f32[128,1408]{1,0:T(8,128)S(1)} %collective-permute-done.3.pair_ref, f32[128,1408]{1,0:T(8,128)S(1)} %collective-permute-done.4.far_ref, ...), custom_call_target="tpu_custom_call", output_to_operand_aliasing={{}: (5, {})} | custom-call | tf_op jit(solution)/shard_map/pallas_call | solution.py:223
  86.9 15.6 %shard_map.42 = f32[1024,1024]{1,0:T(8,128)} custom-call(s32[1]{0:T(128)} %bitcast.odd_ref, f32[128,1280]{1,0:T(8,128)S(1)} %get-tuple-element.8.own_ref, f32[128,1280]{1,0:T(8,128)S(1)} %collective-permute-done.pair_ref, f32[128,1280]{1,0:T(8,128)S(1)} %collective-permute-done.1.far_ref, ...), custom_call_target="tpu_custom_call", output_to_operand_aliasing={{}: (5, {})} | custom-call | tf_op jit(solution)/shard_map/pallas_call | solution.py:223
  (14 shorter events, 0.2 us)
Async XLA Ops:
  0.7 2.2 %copy-start = (bf16[2048,1024]{1,0:T(8,128)(2,1)S(1)}, bf16[2048,1024]{1,0:T(8,128)(2,1)}, u32[]{:S(2)}) copy-start(bf16[2048,1024]{1,0:T(8,128)(2,1)} %h_ref.3) | copy-start | bytes 12582916
  2.8 0.7 copy-start.1
  7.0 3.7 %collective-permute-start.3 = (f32[128,1408]{1,0:T(8,128)S(1)}, f32[128,1408]{1,0:T(8,128)S(1)}, u32[]{:S(2)}, u32[]{:S(2)}) collective-permute-start(f32[128,1408]{1,0:T(8,128)S(1)} %get-tuple-element.9.own_ref), channel_id=1, source_target_pairs={{0,1},{1,0},{2,3},{3,2},{4,5},{5,4},{6,7},{7,6},{8,9},{9,8},{10,11... | collective-permute-start | bytes 2162696 | tf_op jit(solution)/shard_map/ppermute | solution.py:247
  8.4 4.2 %collective-permute-start = (f32[128,1280]{1,0:T(8,128)S(1)}, f32[128,1280]{1,0:T(8,128)S(1)}, u32[]{:S(2)}, u32[]{:S(2)}) collective-permute-start(f32[128,1280]{1,0:T(8,128)S(1)} %get-tuple-element.8.own_ref), channel_id=1, source_target_pairs={{0,1},{1,0},{2,3},{3,2},{4,5},{5,4},{6,7},{7,6},{8,9},{9,8},{10,11... | collective-permute-start | bytes 1966088 | tf_op jit(solution)/shard_map/ppermute | solution.py:247
  9.6 5.0 %collective-permute-start.9 = (f32[128,1024]{1,0:T(8,128)S(1)}, f32[128,1024]{1,0:T(8,128)}, u32[]{:S(2)}, u32[]{:S(2)}) collective-permute-start(f32[128,1024]{1,0:T(8,128)S(1)} %shard_map.38.own_ref), channel_id=1, source_target_pairs={{0,1},{1,0},{2,3},{3,2},{4,5},{5,4},{6,7},{7,6},{8,9},{9,8},{10,11... | collective-permute-start | bytes 1572872 | tf_op jit(solution)/shard_map/ppermute | solution.py:247
  10.5 7.2 %collective-permute-start.6 = (f32[128,896]{1,0:T(8,128)}, f32[128,896]{1,0:T(8,128)}, u32[]{:S(2)}, u32[]{:S(2)}) collective-permute-start(f32[128,896]{1,0:T(8,128)} %get-tuple-element.10.own_ref), channel_id=1, source_target_pairs={{0,1},{1,0},{2,3},{3,2},{4,5},{5,4},{6,7},{7,6},{8,9},{9,8},{10,11... | collective-permute-start | bytes 1376264 | tf_op jit(solution)/shard_map/ppermute | solution.py:247
  10.7 17.2 %collective-permute-start.4 = (f32[128,1408]{1,0:T(8,128)S(1)}, f32[128,1408]{1,0:T(8,128)S(1)}, u32[]{:S(2)}, u32[]{:S(2)}) collective-permute-start(f32[128,1408]{1,0:T(8,128)S(1)} %add_select_fusion), channel_id=1, source_target_pairs={{0,3},{1,4},{2,5},{3,6},{4,7},{5,8},{6,9},{7,10},{8,11},{9,12},{10... | collective-permute-start | bytes 2162696 | tf_op jit(solution)/shard_map/ppermute | solution.py:249
  12.7 29.3 %collective-permute-start.1 = (f32[128,1280]{1,0:T(8,128)S(1)}, f32[128,1280]{1,0:T(8,128)S(1)}, u32[]{:S(2)}, u32[]{:S(2)}) collective-permute-start(f32[128,1280]{1,0:T(8,128)S(1)} %add_select_fusion.1), channel_id=1, source_target_pairs={{0,3},{1,4},{2,5},{3,6},{4,7},{5,8},{6,9},{7,10},{8,11},{9,12},{10... | collective-permute-start | bytes 1966088 | tf_op jit(solution)/shard_map/ppermute | solution.py:249
  15.8 37.5 %collective-permute-start.10 = (f32[128,1024]{1,0:T(8,128)S(1)}, f32[128,1024]{1,0:T(8,128)S(1)}, u32[]{:S(2)}, u32[]{:S(2)}) collective-permute-start(f32[128,1024]{1,0:T(8,128)S(1)} %add_select_fusion.2), channel_id=1, source_target_pairs={{0,3},{1,4},{2,5},{3,6},{4,7},{5,8},{6,9},{7,10},{8,11},{9,12},{10... | collective-permute-start | bytes 1572872 | tf_op jit(solution)/shard_map/ppermute | solution.py:249
  18.9 44.1 %collective-permute-start.7 = (f32[128,896]{1,0:T(8,128)S(1)}, f32[128,896]{1,0:T(8,128)S(1)}, u32[]{:S(2)}, u32[]{:S(2)}) collective-permute-start(f32[128,896]{1,0:T(8,128)S(1)} %add_select_fusion.3), channel_id=1, source_target_pairs={{0,3},{1,4},{2,5},{3,6},{4,7},{5,8},{6,9},{7,10},{8,11},{9,12},{10... | collective-permute-start | bytes 1376264 | tf_op jit(solution)/shard_map/ppermute | solution.py:249
  27.9 50.3 %collective-permute-start.5 = (f32[128,1408]{1,0:T(8,128)S(1)}, f32[128,1408]{1,0:T(8,128)S(1)}, u32[]{:S(2)}, u32[]{:S(2)}) collective-permute-start(f32[128,1408]{1,0:T(8,128)S(1)} %collective-permute-done.4.far_ref), channel_id=1, source_target_pairs={{1,0},{3,2},{5,4},{7,6},{9,8},{11,10},{13,12},{15,14},{17,16},{19,... | collective-permute-start | bytes 2162696 | tf_op jit(solution)/shard_map/ppermute | solution.py:250
  42.0 44.9 %collective-permute-start.2 = (f32[128,1280]{1,0:T(8,128)S(1)}, f32[128,1280]{1,0:T(8,128)S(1)}, u32[]{:S(2)}, u32[]{:S(2)}) collective-permute-start(f32[128,1280]{1,0:T(8,128)S(1)} %collective-permute-done.1.far_ref), channel_id=1, source_target_pairs={{1,0},{3,2},{5,4},{7,6},{9,8},{11,10},{13,12},{15,14},{17,16},{19,... | collective-permute-start | bytes 1966088 | tf_op jit(solution)/shard_map/ppermute | solution.py:250
  53.2 13.7 %collective-permute-start.11 = (f32[128,1024]{1,0:T(8,128)S(1)}, f32[128,1024]{1,0:T(8,128)S(1)}, u32[]{:S(2)}, u32[]{:S(2)}) collective-permute-start(f32[128,1024]{1,0:T(8,128)S(1)} %collective-permute-done.10.far_ref), channel_id=1, source_target_pairs={{1,0},{3,2},{5,4},{7,6},{9,8},{11,10},{13,12},{15,14},{17,16},{19,... | collective-permute-start | bytes 1572872 | tf_op jit(solution)/shard_map/ppermute | solution.py:250
  63.1 8.8 %collective-permute-start.8 = (f32[128,896]{1,0:T(8,128)S(1)}, f32[128,896]{1,0:T(8,128)S(1)}, u32[]{:S(2)}, u32[]{:S(2)}) collective-permute-start(f32[128,896]{1,0:T(8,128)S(1)} %collective-permute-done.7.far_ref), channel_id=1, source_target_pairs={{1,0},{3,2},{5,4},{7,6},{9,8},{11,10},{13,12},{15,14},{17,16},{19,... | collective-permute-start | bytes 1376264 | tf_op jit(solution)/shard_map/ppermute | solution.py:250

commit v4 on v3

v4 whole, which is shorter than its diff:
```python
import functools
import jax
import jax.numpy as jnp
from jax import lax
from jax.experimental import pallas as pl
from jax.experimental.pallas import tpu as pltpu
from jax.sharding import PartitionSpec as P


LANES = 128
SUBS = 8
MICRO = 32
DEPTH = 512
ROOM = 24 << 20
CUTS = (1, 2, 4)
SETTLE = 2


def parts_of(x):
    out = []
    for _ in range(3):
        out.append(x.astype(jnp.bfloat16))
        x = x - out[-1].astype(jnp.float32)
    return out


def exact_tn(a, b):
    a, b = parts_of(a), parts_of(b)
    order = ((0, 0), (0, 1), (1, 0), (1, 1), (0, 2), (2, 0))
    left = jnp.concatenate([a[i] for i, _ in order], 0)
    right = jnp.concatenate([b[j] for _, j in order], 0)
    return lax.dot_general(left, right, (((0,), (0,)), ((), ())), preferred_element_type=jnp.float32)


def exact_nn(a, b):
    a, b = parts_of(a), parts_of(b)
    order = ((0, 0), (0, 1), (1, 0), (1, 1), (0, 2), (2, 0))
    left = jnp.concatenate([a[i] for i, _ in order], 1)
    right = jnp.concatenate([b[j] for _, j in order], 0)
    return lax.dot_general(left, right, (((1,), (0,)), ((), ())), preferred_element_type=jnp.float32)


def row_of(x, i):
    return jnp.broadcast_to(x[i:i + 1, :], x.shape)


def lane_of(x, j):
    return jnp.take_along_axis(x, jnp.full(x.shape, j, jnp.int32), axis=1)


def eliminate(tiles, first):
    sub = lax.broadcasted_iota(jnp.int32, (SUBS, LANES), 0)
    groups = len(tiles)
    for p in range(groups):
        cols = [[lane_of(tiles[g][0], first + SUBS * p + j) for g in range(p, groups)] for j in range(SUBS)]
        scale, mix = None, None
        for i in range(0, SUBS, 2):
            x, y = cols[i], cols[i + 1]
            aa, ab, bb = row_of(x[0], i), row_of(y[0], i), row_of(y[0], i + 1)
            det = aa * bb - ab * ab
            ra, rd = 1.0 / aa, 1.0 / det
            root = lax.rsqrt(aa)
            tail = aa * root * lax.rsqrt(det)
            skew = ab * ra
            scale = jnp.where(sub == i + 1, tail, root if scale is None else jnp.where(sub == i, root, scale))
            mix = jnp.where(sub == i + 1, skew, 0.0 if mix is None else mix)
            w = jnp.where(sub > i + 1, y[0] * aa - x[0] * ab, 0.0)
            z = jnp.where(sub > i + 1, x[0], 0.0)
            mx = [u * ra for u in (z, *x[1:])]
            mw = [w * rd, *((v - m * ab) * (aa * rd) for v, m in zip(y[1:], mx[1:]))]
            for j in range(i + 2, SUBS):
                own, *rest = cols[j]
                e, f = row_of(own, i), row_of(own, i + 1)
                h = f - skew * e
                if j < i + 4:
                    own = (own - (z * e) * ra) - ((w * (f * aa - e * ab)) * ra) * rd
                else:
                    own = own - mx[0] * e - mw[0] * h
                cols[j] = [own, *(c - u * e - v * h for c, u, v in zip(rest, mx[1:], mw[1:]))]
            for t in range(len(tiles[p])):
                e, f = row_of(tiles[p][t], i), row_of(tiles[p][t], i + 1)
                h = f - skew * e
                for g in range(p, groups):
                    tiles[g][t] = tiles[g][t] - mx[g - p] * e - mw[g - p] * h
        for t in range(len(tiles[p])):
            v = tiles[p][t]
            tiles[p][t] = (v - mix * pltpu.roll(v, 1, 0)) * scale
    return tiles


def factor_diag(d_ref):
    n = d_ref.shape[0]
    for r0 in range(0, n, MICRO):
        tiles = [[d_ref[r0 + SUBS * g:r0 + SUBS * (g + 1), LANES * t:LANES * (t + 1)] for t in range(2)] for g in range(MICRO // SUBS)]
        tiles = eliminate(tiles, r0)
        for g, row in enumerate(tiles):
            for t, tile in enumerate(row):
                d_ref[r0 + SUBS * g:r0 + SUBS * (g + 1), LANES * t:LANES * (t + 1)] = tile
        r1 = r0 + MICRO
        if r1 < n:
            u = d_ref[r0:r1, :]
            d_ref[r1:, :] = d_ref[r1:, :] - exact_tn(u[:, :LANES], u)[r1:]


def groups_of(size):
    edges = [0, *[c for c in CUTS if c * LANES < size], size // LANES]
    return list(zip(edges[:-1], edges[1:]))


def panels(group, size):
    at, out = 0, []
    for r in range(*group):
        width = size - r * LANES
        out.append((r, at, width))
        at += width
    return out, at


def add_grams(groups, h, out_refs):
    size = h.shape[1]
    for group, out_ref in zip(groups, out_refs):
        first, last = group[0] * LANES, group[1] * LANES
        gram = lax.dot_general(h[:, first:last], h[:, first:], (((0,), (0,)), ((), ())), preferred_element_type=jnp.float32)
        for b, at, width in panels(group, size)[0]:
            r = b * LANES - first
            out_ref[:, at:at + width] += gram[r:r + LANES, r:]


def set_priors(groups, prior_ref, out_refs):
    size = prior_ref.shape[1]
    r = lax.broadcasted_iota(jnp.int32, (LANES, LANES), 0)
    c = lax.broadcasted_iota(jnp.int32, (LANES, LANES), 1)
    for group, out_ref in zip(groups, out_refs):
        out_ref[...] = jnp.zeros_like(out_ref)
        for b, at, _ in panels(group, size)[0]:
            diag = jnp.broadcast_to(prior_ref[:, b * LANES:(b + 1) * LANES], (LANES, LANES))
            out_ref[:, at:at + LANES] = jnp.where(r == c, diag, 0.0)


def live_rows(h, left):
    index = lax.broadcasted_iota(jnp.int32, h.shape, 0)
    return jnp.where(index < left, h, jnp.zeros_like(h))


def gram_kernel(groups, fetched, count_ref, h_ref, prior_ref, *refs):
    n = len(groups)
    out_refs, refs = refs[:n], refs[n:]
    depth = min(DEPTH, h_ref.shape[0])
    pieces = h_ref.shape[0] // depth
    rows_ref = h_ref
    if fetched:
        rows_ref, bias_ref, sem = refs
        bias = pltpu.make_async_copy(prior_ref, bias_ref, sem.at[pieces])
        bias.start()

    def fetch(k):
        rows = pl.ds(k * depth, depth)
        return pltpu.make_async_copy(h_ref.at[rows, :], rows_ref.at[rows, :], sem.at[k])

    if fetched:
        for k in range(pieces):
            pl.when(k * depth < count_ref[0])(fetch(k).start)
        bias.wait()
    set_priors(groups, bias_ref if fetched else prior_ref, out_refs)
    for k in range(pieces):
        left = count_ref[0] - k * depth
        rows = slice(k * depth, (k + 1) * depth)
        if fetched:
            pl.when(left > 0)(fetch(k).wait)

        @pl.when(left >= depth)
        def _():
            add_grams(groups, rows_ref[rows, :], out_refs)

        @pl.when(jnp.logical_and(left > 0, left < depth))
        def _():
            add_grams(groups, live_rows(rows_ref[rows, :], left), out_refs)


def gram_rows(groups, fetched, observations, counts, prior):
    capacity, size = observations.shape
    totals = [panels(group, size)[1] for group in groups]
    vmem, smem = pl.BlockSpec(memory_space=pltpu.VMEM), pl.BlockSpec(memory_space=pltpu.SMEM)
    if fetched:
        observations = pltpu.with_memory_space_constraint(observations, pltpu.HBM)
        prior = pltpu.with_memory_space_constraint(prior, pltpu.HBM)
        place = pl.BlockSpec(memory_space=pltpu.HBM)
        scratch = [
            pltpu.VMEM((capacity, size), observations.dtype),
            pltpu.VMEM((1, size), prior.dtype),
            pltpu.SemaphoreType.DMA((1 + max(1, capacity // DEPTH),)),
        ]
    else:
        place, scratch = vmem, []
    return pl.pallas_call(
        functools.partial(gram_kernel, groups, fetched),
        out_shape=[jax.ShapeDtypeStruct((LANES, total), jnp.float32) for total in totals],
        in_specs=[smem, place, place],
        out_specs=[vmem] * len(groups),
        scratch_shapes=scratch,
        compiler_params=pltpu.CompilerParams(vmem_limit_bytes=ROOM),
    )(counts, observations, prior)


def own_sum(odd_ref, own, pair):
    return own + jnp.where(odd_ref[0] > 0, pair, 0.0)


def settle_kernel(groups, odd_ref, *refs):
    n = len(groups)
    owns, pairs, (factor_ref, *outs), (u_ref, sem) = refs[:n], refs[n:2 * n], refs[2 * n:-2], refs[-2:]
    known, width = u_ref.shape
    size = known + width
    fetch = pltpu.make_async_copy(factor_ref.at[pl.ds(0, known), pl.ds(known, width)], u_ref, sem)
    fetch.start()
    fetch.wait()
    for group, own_ref, pair_ref, out_ref in zip(groups, owns, pairs, outs):
        for b, at, w in panels(group, size)[0]:
            s = b * LANES - known
            part = own_sum(odd_ref, own_ref[:, at:at + w], pair_ref[:, at:at + w])
            out_ref[:, at:at + w] = part - exact_tn(u_ref[:, s:s + LANES], u_ref[:, s:])


def settle_rows(groups, size, odd, owns, pairs, factor):
    vmem, smem, f32 = pl.BlockSpec(memory_space=pltpu.VMEM), pl.BlockSpec(memory_space=pltpu.SMEM), jnp.float32
    known = groups[0][0] * LANES
    return pl.pallas_call(
        functools.partial(settle_kernel, groups),
        out_shape=[jax.ShapeDtypeStruct(own.shape, f32) for own in owns],
        in_specs=[smem] + [vmem] * (2 * len(groups)) + [pl.BlockSpec(memory_space=pl.ANY)],
        out_specs=[vmem] * len(groups),
        scratch_shapes=[pltpu.VMEM((known, size - known), f32), pltpu.SemaphoreType.DMA],
        compiler_params=pltpu.CompilerParams(vmem_limit_bytes=ROOM),
        name="settle",
    )(odd, *owns, *pairs, factor)


def factor_kernel(group, known, n_parts, odd_ref, *refs):
    start = group[0] * LANES
    parts, refs = refs[:n_parts], refs[n_parts:]
    if start:
        prev_ref, refs = refs[0], refs[1:]
    out_ref, d_refs, o_ref, sem, *rest = refs
    _, size = o_ref.shape
    if start > known:
        u_ref, = rest
        fetch = pltpu.make_async_copy(prev_ref.at[pl.ds(known, start - known), pl.ds(start, size - start)], u_ref, sem.at[0])
        fetch.start()
    far_ref, near_ref, own_ref, *pair = parts
    own = own_sum(odd_ref, own_ref[...], pair[0][...]) if pair else own_ref[...]
    total = own + far_ref[...] + near_ref[...]
    o_ref[...] = jnp.zeros_like(o_ref)
    r = lax.broadcasted_iota(jnp.int32, (LANES, LANES), 0)
    c = lax.broadcasted_iota(jnp.int32, (LANES, LANES), 1)
    eye = jnp.where(r == c, 1.0, 0.0).astype(jnp.float32)
    if start > known:
        fetch.wait()
    puts = []
    for n, (b, at, width) in enumerate(panels(group, size)[0]):
        s = b * LANES
        top = s - start
        d_ref = d_refs.at[n % 2]

        def left_of(first, last):
            a = total[:, at + first:at + last]
            if start > known:
                a = a - exact_tn(u_ref[:, top:top + LANES], u_ref[:, top + first:top + last])
            if top:
                a = a - exact_tn(o_ref[:top, s:s + LANES], o_ref[:top, s + first:s + last])
            return a

        d_ref[:, :LANES] = left_of(0, LANES)
        d_ref[:, LANES:] = eye
        if width > LANES:
            a = left_of(LANES, width)
        factor_diag(d_ref)
        o_ref[top:top + LANES, s:s + LANES] = jnp.where(r <= c, d_ref[:, :LANES], 0.0)
        if width > LANES:
            inverse = d_ref[:, LANES:]
            o_ref[top:top + LANES, s + LANES:s + 2 * LANES] = exact_nn(inverse, a[:, :LANES])
            if width > 2 * LANES:
                o_ref[top:top + LANES, s + 2 * LANES:] = exact_nn(inverse, a[:, LANES:])
        put = pltpu.make_async_copy(o_ref.at[pl.ds(top, LANES), :], out_ref.at[pl.ds(s, LANES), :], sem.at[1 + n])
        put.start()
        puts.append(put)
    for put in puts:
        put.wait()


def factor_rows(group, known, size, odd, parts, prev):
    start, rows = group[0] * LANES, (group[1] - group[0]) * LANES
    f32 = jnp.float32
    scratch = [pltpu.VMEM((2, LANES, 2 * LANES), f32), pltpu.VMEM((rows, size), f32)]
    scratch.append(pltpu.SemaphoreType.DMA((1 + rows // LANES,)))
    in_specs = [pl.BlockSpec(memory_space=pltpu.SMEM)] + [pl.BlockSpec(memory_space=pltpu.VMEM)] * len(parts)
    args = [odd, *parts]
    aliases = {}
    if start:
        aliases = {len(args): 0}
        in_specs.append(pl.BlockSpec(memory_space=pl.ANY))
        args.append(prev)
    if start > known:
        scratch.append(pltpu.VMEM((start - known, size - start), f32))
    return pl.pallas_call(
        functools.partial(factor_kernel, group, known, len(parts)),
        out_shape=jax.ShapeDtypeStruct((size, size), f32),
        in_specs=in_specs,
        out_specs=pl.BlockSpec(memory_space=pl.ANY),
        scratch_shapes=scratch,
        input_output_aliases=aliases,
        compiler_params=pltpu.CompilerParams(vmem_limit_bytes=ROOM),
    )(*args)


def body(observations, counts, prior):
    size = observations.shape[1]
    steps = lax.axis_size("tm")
    groups = groups_of(size)
    odd = lax.rem(lax.axis_index("tm"), 2)
    swap = [(t, t ^ 1) for t in range(steps)]
    ahead = [(t, t + 3) for t in range(steps - 3)]
    inward = [(t, t - 1) for t in range(1, steps, 2)]
    owns = []
    for i, share in enumerate((groups[:1], groups[1:])):
        owns += gram_rows(share, i == 0, observations, counts, prior)
    parts = []
    for own in owns:
        pair = lax.ppermute(own, "tm", swap)
        send = jnp.where(odd == 0, own + pair, own)
        far = lax.ppermute(send, "tm", ahead)
        near = lax.ppermute(far, "tm", inward)
        parts.append([far, near, own, pair])
    factor, known = None, 0
    for i, group in enumerate(groups):
        if i == SETTLE:
            known = group[0] * LANES
            owns, pairs = zip(*(part[2:] for part in parts[i:]))
            settled = settle_rows(groups[i:], size, odd[None], owns, pairs, factor)
            parts[i:] = [[*part[:2], base] for part, base in zip(parts[i:], settled)]
        factor = factor_rows(group, known, size, odd[None], parts[i], factor)
    return factor[None]


def solution(mesh):
    placed = (P(("grp", "tm"), None), P(("grp", "tm")), P(("grp", "tm"), None))
    return jax.shard_map(
        body, mesh=mesh, in_specs=placed, out_specs=P(("grp", "tm"), None, None), check_vma=False
    )
```

time: 103 us -> 105 us (1.019)
  the two profiles are of different devices: /device:TPU:21 before, /device:TPU:25 now
where the time goes in v4:
time: 105 us; the launch traced here: 104 us
  waiting for transfers between devices  46.4 us (44%)
  Pallas kernels  37.4 us (36%)
  starting transfers between devices  11.9 us (11%)
  local copies, waits for them, and re-layouts  5.05 us (5%)
  other arithmetic  2.45 us (2%)
    ppermute x4, waiting for transfers between devices, body(): far = lax.ppermute(send, 'tm', ahead)  46.4 us
    pallas_call x4, Pallas kernels, factor_rows(): pl.pallas_call(functools.partial(factor_kernel, group, known, len(parts))...  32.4 us
    ppermute x4, starting transfers between devices, body(): near = lax.ppermute(far, 'tm', inward)  5.44 us
    ppermute x4, starting transfers between devices, body(): far = lax.ppermute(send, 'tm', ahead)  5.17 us
    unnamed x6, local copies, waits for them, and re-layouts  5.05 us
    pallas_call x2, Pallas kernels, gram_rows(): pl.pallas_call(functools.partial(gram_kernel, groups, fetched), out_shape...  3.43 us
    select_n x4, other arithmetic, body(): send = jnp.where(odd == 0, own + pair, own)  2.45 us
  transfers between devices with their start and end apart: 12, of which 4 were waited for; matrix products, arithmetic and copies ran while one was open for 2% of the time, Pallas kernels for 21%

profile of v4, /device:TPU:25, one launch (start us, length us, event | category | flops | bytes accessed | tf_op | source)
XLA Modules:
  0.0 104.3 jit_solution(6508259368667489663)
XLA Ops:
  0.7 2.2 %copy-done.1 = bf16[2048,1024]{1,0:T(8,128)(2,1)S(1)} copy-done((bf16[2048,1024]{1,0:T(8,128)(2,1)S(1)}, bf16[2048,1024]{1,0:T(8,128)(2,1)}, u32[]{:S(2)}) %copy-start.1) | copy-done | bytes 4194328
  2.8 0.7 copy-done.2
  3.5 1.8 %shard_map.37 = (f32[128,896]{1,0:T(8,128)}, f32[128,1408]{1,0:T(8,128)S(1)}, f32[128,1280]{1,0:T(8,128)S(1)}) custom-call(s32[1]{0:T(128)S(6)} %copy.10.count_ref, bf16[2048,1024]{1,0:T(8,128)(2,1)S(1)} %copy-done.1, f32[1,1024]{1,0:T(1,128)S(1)} %copy-done.2), custom_call_target="tpu_custom_call" | custom-call | tf_op jit(solution)/shard_map/pallas_call | solution.py:195
  6.0 1.7 %shard_map.38.refs_2_ = f32[128,1024]{1,0:T(8,128)S(1)} custom-call(s32[1]{0:T(128)S(6)} %copy.10.count_ref, bf16[2048,1024]{1,0:T(8,128)(2,1)} %h_ref.3, f32[1,1024]{1,0:T(1,128)} %prior_ref.3), custom_call_target="tpu_custom_call" | custom-call | tf_op jit(solution)/shard_map/pallas_call | solution.py:195
  8.4 1.3 %collective-permute-start.10 = (f32[128,1408]{1,0:T(8,128)S(1)}, f32[128,1408]{1,0:T(8,128)S(1)}, u32[]{:S(2)}, u32[]{:S(2)}) collective-permute-start(f32[128,1408]{1,0:T(8,128)S(1)} %add_select_fusion), channel_id=1, source_target_pairs={{0,3},{1,4},{2,5},{3,6},{4,7},{5,8},{6,9},{7,10},{8,11},{9,12},{10... | collective-permute-start | bytes 2162696 | tf_op jit(solution)/shard_map/ppermute | solution.py:330
  9.8 1.3 %collective-permute-start.1 = (f32[128,1280]{1,0:T(8,128)S(1)}, f32[128,1280]{1,0:T(8,128)S(1)}, u32[]{:S(2)}, u32[]{:S(2)}) collective-permute-start(f32[128,1280]{1,0:T(8,128)S(1)} %add_select_fusion.1), channel_id=1, source_target_pairs={{0,3},{1,4},{2,5},{3,6},{4,7},{5,8},{6,9},{7,10},{8,11},{9,12},{10... | collective-permute-start | bytes 1966088 | tf_op jit(solution)/shard_map/ppermute | solution.py:330
  11.1 1.1 %add_select_fusion.2 = f32[128,1024]{1,0:T(8,128)S(1)} fusion(f32[128,1024]{1,0:T(8,128)S(1)} %shard_map.38.refs_2_, f32[128,1024]{1,0:T(8,128)} %collective-permute-done.7.refs_3_, pred[]{:T(512)S(6)} %eq.2), kind=kLoop, calls=%fused_computation.2 | loop fusion | flops 262144 | bytes 1572865 | tf_op jit(solution)/shard_map/jit(_where)/select_n | solution.py:329
  12.2 1.3 %collective-permute-start.8 = (f32[128,1024]{1,0:T(8,128)S(1)}, f32[128,1024]{1,0:T(8,128)S(1)}, u32[]{:S(2)}, u32[]{:S(2)}) collective-permute-start(f32[128,1024]{1,0:T(8,128)S(1)} %add_select_fusion.2), channel_id=1, source_target_pairs={{0,3},{1,4},{2,5},{3,6},{4,7},{5,8},{6,9},{7,10},{8,11},{9,12},{10... | collective-permute-start | bytes 1572872 | tf_op jit(solution)/shard_map/ppermute | solution.py:330
  13.5 1.2 %add_select_fusion.3 = f32[128,896]{1,0:T(8,128)S(1)} fusion(f32[128,896]{1,0:T(8,128)} %get-tuple-element.12.refs_2_, f32[128,896]{1,0:T(8,128)} %collective-permute-done.4.refs_3_, pred[]{:T(512)S(6)} %eq.2), kind=kLoop, calls=%fused_computation.3 | loop fusion | flops 229376 | bytes 1376257 | tf_op jit(solution)/shard_map/jit(_where)/select_n | solution.py:329
  14.7 1.3 %collective-permute-start.5 = (f32[128,896]{1,0:T(8,128)S(1)}, f32[128,896]{1,0:T(8,128)S(1)}, u32[]{:S(2)}, u32[]{:S(2)}) collective-permute-start(f32[128,896]{1,0:T(8,128)S(1)} %add_select_fusion.3), channel_id=1, source_target_pairs={{0,3},{1,4},{2,5},{3,6},{4,7},{5,8},{6,9},{7,10},{8,11},{9,12},{10... | collective-permute-start | bytes 1376264 | tf_op jit(solution)/shard_map/ppermute | solution.py:330
  16.0 15.9 %collective-permute-done.10.refs_0_ = f32[128,1408]{1,0:T(8,128)S(1)} collective-permute-done((f32[128,1408]{1,0:T(8,128)S(1)}, f32[128,1408]{1,0:T(8,128)S(1)}, u32[]{:S(2)}, u32[]{:S(2)}) %collective-permute-start.10) | collective-permute-done | bytes 720928 | tf_op jit(solution)/shard_map/ppermute | solution.py:330
  31.9 1.3 %collective-permute-start.11 = (f32[128,1408]{1,0:T(8,128)S(1)}, f32[128,1408]{1,0:T(8,128)S(1)}, u32[]{:S(2)}, u32[]{:S(2)}) collective-permute-start(f32[128,1408]{1,0:T(8,128)S(1)} %collective-permute-done.10.refs_0_), channel_id=1, source_target_pairs={{1,0},{3,2},{5,4},{7,6},{9,8},{11,10},{13,12},{15,14},{17,16},{19,... | collective-permute-start | bytes 2162696 | tf_op jit(solution)/shard_map/ppermute | solution.py:331
  33.2 12.7 %collective-permute-done.1.refs_0_ = f32[128,1280]{1,0:T(8,128)S(1)} collective-permute-done((f32[128,1280]{1,0:T(8,128)S(1)}, f32[128,1280]{1,0:T(8,128)S(1)}, u32[]{:S(2)}, u32[]{:S(2)}) %collective-permute-start.1) | collective-permute-done | bytes 655392 | tf_op jit(solution)/shard_map/ppermute | solution.py:330
  45.9 1.3 %collective-permute-start.2 = (f32[128,1280]{1,0:T(8,128)S(1)}, f32[128,1280]{1,0:T(8,128)S(1)}, u32[]{:S(2)}, u32[]{:S(2)}) collective-permute-start(f32[128,1280]{1,0:T(8,128)S(1)} %collective-permute-done.1.refs_0_), channel_id=1, source_target_pairs={{1,0},{3,2},{5,4},{7,6},{9,8},{11,10},{13,12},{15,14},{17,16},{19,... | collective-permute-start | bytes 1966088 | tf_op jit(solution)/shard_map/ppermute | solution.py:331
  47.2 9.9 %collective-permute-done.8.refs_0_ = f32[128,1024]{1,0:T(8,128)S(1)} collective-permute-done((f32[128,1024]{1,0:T(8,128)S(1)}, f32[128,1024]{1,0:T(8,128)S(1)}, u32[]{:S(2)}, u32[]{:S(2)}) %collective-permute-start.8) | collective-permute-done | bytes 524320 | tf_op jit(solution)/shard_map/ppermute | solution.py:330
  57.1 1.3 %collective-permute-start.9 = (f32[128,1024]{1,0:T(8,128)S(1)}, f32[128,1024]{1,0:T(8,128)S(1)}, u32[]{:S(2)}, u32[]{:S(2)}) collective-permute-start(f32[128,1024]{1,0:T(8,128)S(1)} %collective-permute-done.8.refs_0_), channel_id=1, source_target_pairs={{1,0},{3,2},{5,4},{7,6},{9,8},{11,10},{13,12},{15,14},{17,16},{19,... | collective-permute-start | bytes 1572872 | tf_op jit(solution)/shard_map/ppermute | solution.py:331
  58.5 7.9 %collective-permute-done.5.refs_0_ = f32[128,896]{1,0:T(8,128)S(1)} collective-permute-done((f32[128,896]{1,0:T(8,128)S(1)}, f32[128,896]{1,0:T(8,128)S(1)}, u32[]{:S(2)}, u32[]{:S(2)}) %collective-permute-start.5) | collective-permute-done | bytes 458784 | tf_op jit(solution)/shard_map/ppermute | solution.py:330
  66.4 1.5 %collective-permute-start.6 = (f32[128,896]{1,0:T(8,128)S(1)}, f32[128,896]{1,0:T(8,128)S(1)}, u32[]{:S(2)}, u32[]{:S(2)}) collective-permute-start(f32[128,896]{1,0:T(8,128)S(1)} %collective-permute-done.5.refs_0_), channel_id=1, source_target_pairs={{1,0},{3,2},{5,4},{7,6},{9,8},{11,10},{13,12},{15,14},{17,16},{19,... | collective-permute-start | bytes 1376264 | tf_op jit(solution)/shard_map/ppermute | solution.py:331
  67.9 4.9 %shard_map.39.refs_4_ = f32[1024,1024]{1,0:T(8,128)} custom-call(s32[1]{0:T(128)} %bitcast.odd_ref, f32[128,1024]{1,0:T(8,128)S(1)} %collective-permute-done.8.refs_0_, f32[128,1024]{1,0:T(8,128)S(1)} %collective-permute-done.9.refs_1_, f32[128,1024]{1,0:T(8,128)S(1)} %shard_map.38.refs_2_, f32[128,1024]{1,0:T(8,128)} %collective-permute-done.7.refs_3_), custom_call_target="tpu_custom_call" | custom-call | tf_op jit(solution)/shard_map/pallas_call | solution.py:304
  72.8 6.4 %shard_map.40.refs_4_.refs_3_ = f32[1024,1024]{1,0:T(8,128)} custom-call(s32[1]{0:T(128)} %bitcast.odd_ref, f32[128,896]{1,0:T(8,128)S(1)} %collective-permute-done.5.refs_0_, f32[128,896]{1,0:T(8,128)S(1)} %collective-permute-done.6.refs_1_, f32[128,896]{1,0:T(8,128)} %get-tuple-element.12.refs_2_, ...), custom_call_target="tpu_custom_call", output_to_operand_aliasing={{}: (5, {})} | custom-call | tf_op jit(solution)/shard_map/pallas_call | solution.py:304
  79.2 2.2 %copy-done = f32[1024,1024]{1,0:T(8,128)S(1)} copy-done((f32[1024,1024]{1,0:T(8,128)S(1)}, f32[1024,1024]{1,0:T(8,128)}, u32[]{:S(2)}) %copy-start) | copy-done | bytes 4194328
  81.4 1.6 %settle.1 = (f32[128,1408]{1,0:T(8,128)S(1)}, f32[128,1280]{1,0:T(8,128)S(1)}) custom-call(s32[1]{0:T(128)} %bitcast.odd_ref, f32[128,1408]{1,0:T(8,128)S(1)} %get-tuple-element.11.refs_0_, f32[128,1280]{1,0:T(8,128)S(1)} %get-tuple-element.10.refs_1_, f32[128,1408]{1,0:T(8,128)S(1)} %collective-permute-done.3.refs_2_, ...), custom_call_target="tpu_custom_call" | custom-call | tf_op jit(solution)/shard_map/settle/pallas_call | solution.py:227
  83.0 6.9 %shard_map.41.refs_3_ = f32[1024,1024]{1,0:T(8,128)} custom-call(s32[1]{0:T(128)} %bitcast.odd_ref, f32[128,1408]{1,0:T(8,128)S(1)} %collective-permute-done.10.refs_0_, f32[128,1408]{1,0:T(8,128)S(1)} %collective-permute-done.11.refs_1_, f32[128,1408]{1,0:T(8,128)S(1)} %get-tuple-element.14.refs_2_, ...), custom_call_target="tpu_custom_call", output_to_operand_aliasing={{}: (4, {})} | custom-call | tf_op jit(solution)/shard_map/pallas_call | solution.py:304
  89.9 14.2 %shard_map.42 = f32[1024,1024]{1,0:T(8,128)} custom-call(s32[1]{0:T(128)} %bitcast.odd_ref, f32[128,1280]{1,0:T(8,128)S(1)} %collective-permute-done.1.refs_0_, f32[128,1280]{1,0:T(8,128)S(1)} %collective-permute-done.2.refs_1_, f32[128,1280]{1,0:T(8,128)S(1)} %get-tuple-element.13.refs_2_, ...), custom_call_target="tpu_custom_call", output_to_operand_aliasing={{}: (4, {})} | custom-call | tf_op jit(solution)/shard_map/pallas_call | solution.py:304
  (17 shorter events, 1.5 us)
Async XLA Ops:
  0.7 2.2 %copy-start.1 = (bf16[2048,1024]{1,0:T(8,128)(2,1)S(1)}, bf16[2048,1024]{1,0:T(8,128)(2,1)}, u32[]{:S(2)}) copy-start(bf16[2048,1024]{1,0:T(8,128)(2,1)} %h_ref.3) | copy-start | bytes 12582916
  2.8 0.7 copy-start.2
  5.3 3.0 %collective-permute-start.3 = (f32[128,1408]{1,0:T(8,128)S(1)}, f32[128,1408]{1,0:T(8,128)S(1)}, u32[]{:S(2)}, u32[]{:S(2)}) collective-permute-start(f32[128,1408]{1,0:T(8,128)S(1)} %get-tuple-element.11.refs_0_), channel_id=1, source_target_pairs={{0,1},{1,0},{2,3},{3,2},{4,5},{5,4},{6,7},{7,6},{8,9},{9,8},{10,11... | collective-permute-start | bytes 2162696 | tf_op jit(solution)/shard_map/ppermute | solution.py:328
  6.0 3.7 %collective-permute-start = (f32[128,1280]{1,0:T(8,128)S(1)}, f32[128,1280]{1,0:T(8,128)S(1)}, u32[]{:S(2)}, u32[]{:S(2)}) collective-permute-start(f32[128,1280]{1,0:T(8,128)S(1)} %get-tuple-element.10.refs_1_), channel_id=1, source_target_pairs={{0,1},{1,0},{2,3},{3,2},{4,5},{5,4},{6,7},{7,6},{8,9},{9,8},{10,11... | collective-permute-start | bytes 1966088 | tf_op jit(solution)/shard_map/ppermute | solution.py:328
  7.6 3.4 %collective-permute-start.7 = (f32[128,1024]{1,0:T(8,128)S(1)}, f32[128,1024]{1,0:T(8,128)}, u32[]{:S(2)}, u32[]{:S(2)}) collective-permute-start(f32[128,1024]{1,0:T(8,128)S(1)} %shard_map.38.refs_2_), channel_id=1, source_target_pairs={{0,1},{1,0},{2,3},{3,2},{4,5},{5,4},{6,7},{7,6},{8,9},{9,8},{10,11... | collective-permute-start | bytes 1572872 | tf_op jit(solution)/shard_map/ppermute | solution.py:328
  8.2 5.3 %collective-permute-start.4 = (f32[128,896]{1,0:T(8,128)}, f32[128,896]{1,0:T(8,128)}, u32[]{:S(2)}, u32[]{:S(2)}) collective-permute-start(f32[128,896]{1,0:T(8,128)} %get-tuple-element.12.refs_2_), channel_id=1, source_target_pairs={{0,1},{1,0},{2,3},{3,2},{4,5},{5,4},{6,7},{7,6},{8,9},{9,8},{10,11... | collective-permute-start | bytes 1376264 | tf_op jit(solution)/shard_map/ppermute | solution.py:328
  8.4 23.5 %collective-permute-start.10 = (f32[128,1408]{1,0:T(8,128)S(1)}, f32[128,1408]{1,0:T(8,128)S(1)}, u32[]{:S(2)}, u32[]{:S(2)}) collective-permute-start(f32[128,1408]{1,0:T(8,128)S(1)} %add_select_fusion), channel_id=1, source_target_pairs={{0,3},{1,4},{2,5},{3,6},{4,7},{5,8},{6,9},{7,10},{8,11},{9,12},{10... | collective-permute-start | bytes 2162696 | tf_op jit(solution)/shard_map/ppermute | solution.py:330
  9.8 36.1 %collective-permute-start.1 = (f32[128,1280]{1,0:T(8,128)S(1)}, f32[128,1280]{1,0:T(8,128)S(1)}, u32[]{:S(2)}, u32[]{:S(2)}) collective-permute-start(f32[128,1280]{1,0:T(8,128)S(1)} %add_select_fusion.1), channel_id=1, source_target_pairs={{0,3},{1,4},{2,5},{3,6},{4,7},{5,8},{6,9},{7,10},{8,11},{9,12},{10... | collective-permute-start | bytes 1966088 | tf_op jit(solution)/shard_map/ppermute | solution.py:330
  12.2 45.0 %collective-permute-start.8 = (f32[128,1024]{1,0:T(8,128)S(1)}, f32[128,1024]{1,0:T(8,128)S(1)}, u32[]{:S(2)}, u32[]{:S(2)}) collective-permute-start(f32[128,1024]{1,0:T(8,128)S(1)} %add_select_fusion.2), channel_id=1, source_target_pairs={{0,3},{1,4},{2,5},{3,6},{4,7},{5,8},{6,9},{7,10},{8,11},{9,12},{10... | collective-permute-start | bytes 1572872 | tf_op jit(solution)/shard_map/ppermute | solution.py:330
  14.7 51.7 %collective-permute-start.5 = (f32[128,896]{1,0:T(8,128)S(1)}, f32[128,896]{1,0:T(8,128)S(1)}, u32[]{:S(2)}, u32[]{:S(2)}) collective-permute-start(f32[128,896]{1,0:T(8,128)S(1)} %add_select_fusion.3), channel_id=1, source_target_pairs={{0,3},{1,4},{2,5},{3,6},{4,7},{5,8},{6,9},{7,10},{8,11},{9,12},{10... | collective-permute-start | bytes 1376264 | tf_op jit(solution)/shard_map/ppermute | solution.py:330
  31.9 51.1 %collective-permute-start.11 = (f32[128,1408]{1,0:T(8,128)S(1)}, f32[128,1408]{1,0:T(8,128)S(1)}, u32[]{:S(2)}, u32[]{:S(2)}) collective-permute-start(f32[128,1408]{1,0:T(8,128)S(1)} %collective-permute-done.10.refs_0_), channel_id=1, source_target_pairs={{1,0},{3,2},{5,4},{7,6},{9,8},{11,10},{13,12},{15,14},{17,16},{19,... | collective-permute-start | bytes 2162696 | tf_op jit(solution)/shard_map/ppermute | solution.py:331
  45.9 44.0 %collective-permute-start.2 = (f32[128,1280]{1,0:T(8,128)S(1)}, f32[128,1280]{1,0:T(8,128)S(1)}, u32[]{:S(2)}, u32[]{:S(2)}) collective-permute-start(f32[128,1280]{1,0:T(8,128)S(1)} %collective-permute-done.1.refs_0_), channel_id=1, source_target_pairs={{1,0},{3,2},{5,4},{7,6},{9,8},{11,10},{13,12},{15,14},{17,16},{19,... | collective-permute-start | bytes 1966088 | tf_op jit(solution)/shard_map/ppermute | solution.py:331
  57.1 10.7 %collective-permute-start.9 = (f32[128,1024]{1,0:T(8,128)S(1)}, f32[128,1024]{1,0:T(8,128)S(1)}, u32[]{:S(2)}, u32[]{:S(2)}) collective-permute-start(f32[128,1024]{1,0:T(8,128)S(1)} %collective-permute-done.8.refs_0_), channel_id=1, source_target_pairs={{1,0},{3,2},{5,4},{7,6},{9,8},{11,10},{13,12},{15,14},{17,16},{19,... | collective-permute-start | bytes 1572872 | tf_op jit(solution)/shard_map/ppermute | solution.py:331
  66.4 6.4 %collective-permute-start.6 = (f32[128,896]{1,0:T(8,128)S(1)}, f32[128,896]{1,0:T(8,128)S(1)}, u32[]{:S(2)}, u32[]{:S(2)}) collective-permute-start(f32[128,896]{1,0:T(8,128)S(1)} %collective-permute-done.5.refs_0_), channel_id=1, source_target_pairs={{1,0},{3,2},{5,4},{7,6},{9,8},{11,10},{13,12},{15,14},{17,16},{19,... | collective-permute-start | bytes 1376264 | tf_op jit(solution)/shard_map/ppermute | solution.py:331
  79.2 2.2 %copy-start = (f32[1024,1024]{1,0:T(8,128)S(1)}, f32[1024,1024]{1,0:T(8,128)}, u32[]{:S(2)}) copy-start(f32[1024,1024]{1,0:T(8,128)} %shard_map.40.refs_4_.refs_3_) | copy-start | bytes 12582916

commit v5 on v4

--- a/solution.py
+++ b/solution.py
@@ -10,9 +10,10 @@
 LANES = 128
 SUBS = 8
 MICRO = 32
+LEAD = 3
 DEPTH = 512
 ROOM = 24 << 20
-CUTS = (1, 2, 4)
+CUTS = (1, 2, 4, 5)
 SETTLE = 2
 
 
@@ -52,7 +53,11 @@
     sub = lax.broadcasted_iota(jnp.int32, (SUBS, LANES), 0)
     groups = len(tiles)
     for p in range(groups):
-        cols = [[lane_of(tiles[g][0], first + SUBS * p + j) for g in range(p, groups)] for j in range(SUBS)]
+        base = first + SUBS * p
+        cols = [[lane_of(tiles[g][0], base + j) for g in range(p + (p > 0), groups)] for j in range(SUBS)]
+        if p:
+            cols = [[own, *rest] for own, rest in zip(coming, cols)]
+        last = p + 1 == groups
         scale, mix = None, None
         for i in range(0, SUBS, 2):
             x, y = cols[i], cols[i + 1]
@@ -77,6 +82,16 @@
                 else:
                     own = own - mx[0] * e - mw[0] * h
                 cols[j] = [own, *(c - u * e - v * h for c, u, v in zip(rest, mx[1:], mw[1:]))]
+            if not last and i == SUBS - 2 * LEAD:
+                coming = [lane_of(tiles[p + 1][0], base + SUBS + j) for j in range(SUBS)]
+                over = [lane_of(tiles[p][0], base + SUBS + j) for j in range(SUBS)]
+            if not last and i >= SUBS - 2 * LEAD:
+                for j in range(SUBS):
+                    e, f = row_of(over[j], i), row_of(over[j], i + 1)
+                    h = f - skew * e
+                    coming[j] = coming[j] - mx[1] * e - mw[1] * h
+                    if i + 2 < SUBS:
+                        over[j] = over[j] - mx[0] * e - mw[0] * h
             for t in range(len(tiles[p])):
                 e, f = row_of(tiles[p][t], i), row_of(tiles[p][t], i + 1)
                 h = f - skew * e
@@ -89,9 +104,9 @@
 
 
 def factor_diag(d_ref):
-    n = d_ref.shape[0]
+    n, wide = d_ref.shape
     for r0 in range(0, n, MICRO):
-        tiles = [[d_ref[r0 + SUBS * g:r0 + SUBS * (g + 1), LANES * t:LANES * (t + 1)] for t in range(2)] for g in range(MICRO // SUBS)]
+        tiles = [[d_ref[r0 + SUBS * g:r0 + SUBS * (g + 1), LANES * t:LANES * (t + 1)] for t in range(wide // LANES)] for g in range(MICRO // SUBS)]
         tiles = eliminate(tiles, r0)
         for g, row in enumerate(tiles):
             for t, tile in enumerate(row):
@@ -235,12 +250,13 @@
     )(odd, *owns, *pairs, factor)
 
 
-def factor_kernel(group, known, n_parts, odd_ref, *refs):
+def factor_kernel(group, later, known, n_parts, odd_ref, *refs):
     start = group[0] * LANES
-    parts, refs = refs[:n_parts], refs[n_parts:]
+    parts, bases, refs = refs[:n_parts], refs[n_parts:n_parts + len(later)], refs[n_parts + len(later):]
     if start:
         prev_ref, refs = refs[0], refs[1:]
-    out_ref, d_refs, o_ref, sem, *rest = refs
+    out_ref, lowered, refs = refs[0], refs[1:1 + len(later)], refs[1 + len(later):]
+    d_refs, o_ref, sem, *rest = refs
     _, size = o_ref.shape
     if start > known:
         u_ref, = rest
@@ -270,10 +286,12 @@
             return a
 
         d_ref[:, :LANES] = left_of(0, LANES)
-        d_ref[:, LANES:] = eye
         if width > LANES:
+            d_ref[:, LANES:] = eye
             a = left_of(LANES, width)
-        factor_diag(d_ref)
+            factor_diag(d_ref)
+        else:
+            factor_diag(d_ref.at[:, pl.ds(0, LANES)])
         o_ref[top:top + LANES, s:s + LANES] = jnp.where(r <= c, d_ref[:, :LANES], 0.0)
         if width > LANES:
             inverse = d_ref[:, LANES:]
@@ -283,17 +301,21 @@
         put = pltpu.make_async_copy(o_ref.at[pl.ds(top, LANES), :], out_ref.at[pl.ds(s, LANES), :], sem.at[1 + n])
         put.start()
         puts.append(put)
+    for below, base_ref, low_ref in zip(later, bases, lowered):
+        for b, at, w in panels(below, size)[0]:
+            s = b * LANES
+            low_ref[:, at:at + w] = base_ref[:, at:at + w] - exact_tn(o_ref[:, s:s + LANES], o_ref[:, s:])
     for put in puts:
         put.wait()
 
 
-def factor_rows(group, known, size, odd, parts, prev):
+def factor_rows(group, later, known, size, odd, parts, bases, prev):
     start, rows = group[0] * LANES, (group[1] - group[0]) * LANES
     f32 = jnp.float32
     scratch = [pltpu.VMEM((2, LANES, 2 * LANES), f32), pltpu.VMEM((rows, size), f32)]
     scratch.append(pltpu.SemaphoreType.DMA((1 + rows // LANES,)))
-    in_specs = [pl.BlockSpec(memory_space=pltpu.SMEM)] + [pl.BlockSpec(memory_space=pltpu.VMEM)] * len(parts)
-    args = [odd, *parts]
+    in_specs = [pl.BlockSpec(memory_space=pltpu.SMEM)] + [pl.BlockSpec(memory_space=pltpu.VMEM)] * (len(parts) + len(bases))
+    args = [odd, *parts, *bases]
     aliases = {}
     if start:
         aliases = {len(args): 0}
@@ -302,10 +324,10 @@
     if start > known:
         scratch.append(pltpu.VMEM((start - known, size - start), f32))
     return pl.pallas_call(
-        functools.partial(factor_kernel, group, known, len(parts)),
-        out_shape=jax.ShapeDtypeStruct((size, size), f32),
+        functools.partial(factor_kernel, group, later, known, len(parts)),
+        out_shape=[jax.ShapeDtypeStruct((size, size), f32)] + [jax.ShapeDtypeStruct(base.shape, f32) for base in bases],
         in_specs=in_specs,
-        out_specs=pl.BlockSpec(memory_space=pl.ANY),
+        out_specs=[pl.BlockSpec(memory_space=pl.ANY)] + [pl.BlockSpec(memory_space=pltpu.VMEM)] * len(bases),
         scratch_shapes=scratch,
         input_output_aliases=aliases,
         compiler_params=pltpu.CompilerParams(vmem_limit_bytes=ROOM),
@@ -337,7 +359,12 @@
             owns, pairs = zip(*(part[2:] for part in parts[i:]))
             settled = settle_rows(groups[i:], size, odd[None], owns, pairs, factor)
             parts[i:] = [[*part[:2], base] for part, base in zip(parts[i:], settled)]
-        factor = factor_rows(group, known, size, odd[None], parts[i], factor)
+        later = groups[i + 1:] if i >= SETTLE else []
+        bases = [part[2] for part in parts[i + 1:]] if later else []
+        factor, *lowered = factor_rows(group, later, known, size, odd[None], parts[i], bases, factor)
+        if later:
+            known = group[1] * LANES
+            parts[i + 1:] = [[*part[:2], low] for part, low in zip(parts[i + 1:], lowered)]
     return factor[None]
 
 

time: 105 us -> 102 us (0.971)
  Pallas kernels: 37.4 us -> 34.3 us
  starting transfers between devices: 11.9 us -> 14.9 us
  waiting for transfers between devices: 46.4 us -> 43.5 us
    pallas_call x4 -> x5, Pallas kernels: 32.4 us -> 28 us  [factor_rows(): pl.pallas_call(functools.partial(factor_kernel, group, later, known, len(...]
    ppermute x4 -> x5, waiting for transfers between devices: 46.4 us -> 43.4 us  [body(): far = lax.ppermute(send, 'tm', ahead)]
    ppermute x4 -> x5, starting transfers between devices: 5.17 us -> 6.46 us  [body(): far = lax.ppermute(send, 'tm', ahead)]
    ppermute x4 -> x5, starting transfers between devices: 5.44 us -> 6.73 us  [body(): near = lax.ppermute(far, 'tm', inward)]
    pallas_call x1, Pallas kernels: 1.55 us -> 2.82 us  [settle_rows(): pl.pallas_call(functools.partial(settle_kernel, groups), out_shape=[jax.S...]
    select_n x4 -> x5, other arithmetic: 2.45 us -> 2.41 us  [body(): send = jnp.where(odd == 0, own + pair, own)]
  transfers between devices with their start and end apart: 12 -> 15, of which waited for: 4 -> 4; matrix products, arithmetic and copies ran while one was open for 2% -> 2% of each run, Pallas kernels for 21% -> 23%
where the time goes in v5:
time: 102 us; the launch traced here: 101 us
  waiting for transfers between devices  43.5 us (43%)
  Pallas kernels  34.3 us (34%)
  starting transfers between devices  14.9 us (15%)
  local copies, waits for them, and re-layouts  5.05 us (5%)
  other arithmetic  2.41 us (2%)
  between operations  1.1 us (1%)
    ppermute x5, waiting for transfers between devices, body(): far = lax.ppermute(send, 'tm', ahead)  43.4 us
    pallas_call x5, Pallas kernels, factor_rows(): pl.pallas_call(functools.partial(factor_kernel, group, later, known, len(...  28 us
    ppermute x5, starting transfers between devices, body(): near = lax.ppermute(far, 'tm', inward)  6.73 us
    ppermute x5, starting transfers between devices, body(): far = lax.ppermute(send, 'tm', ahead)  6.46 us
    unnamed x6, local copies, waits for them, and re-layouts  5.05 us
    pallas_call x2, Pallas kernels, gram_rows(): pl.pallas_call(functools.partial(gram_kernel, groups, fetched), out_shape...  3.5 us
    pallas_call x1, Pallas kernels, settle_rows(): pl.pallas_call(functools.partial(settle_kernel, groups), out_shape=[jax.S...  2.82 us
    select_n x5, other arithmetic, body(): send = jnp.where(odd == 0, own + pair, own)  2.41 us
  transfers between devices with their start and end apart: 15, of which 4 were waited for; matrix products, arithmetic and copies ran while one was open for 2% of the time, Pallas kernels for 23%

profile of v5, /device:TPU:25, one launch (start us, length us, event | category | flops | bytes accessed | tf_op | source)
XLA Modules:
  0.0 101.3 jit_solution(10507185532538816098)
XLA Ops:
  0.7 2.2 %copy-done.1 = bf16[2048,1024]{1,0:T(8,128)(2,1)S(1)} copy-done((bf16[2048,1024]{1,0:T(8,128)(2,1)S(1)}, bf16[2048,1024]{1,0:T(8,128)(2,1)}, u32[]{:S(2)}) %copy-start.1) | copy-done | bytes 4194328
  3.5 1.8 %shard_map.37 = (f32[128,896]{1,0:T(8,128)S(1)}, f32[128,1408]{1,0:T(8,128)S(1)}, f32[128,512]{1,0:T(8,128)}, f32[128,768]{1,0:T(8,128)}) custom-call(s32[1]{0:T(128)S(6)} %copy.12.count_ref, bf16[2048,1024]{1,0:T(8,128)(2,1)S(1)} %copy-done.1, f32[1,1024]{1,0:T(1,128)S(1)} %copy-done.2), custom_call_target="tpu_custom_call" | custom-call | tf_op jit(solution)/shard_map/pallas_call | solution.py:210
  6.0 1.7 %shard_map.38.refs_2_ = f32[128,1024]{1,0:T(8,128)S(1)} custom-call(s32[1]{0:T(128)S(6)} %copy.12.count_ref, bf16[2048,1024]{1,0:T(8,128)(2,1)} %h_ref.3, f32[1,1024]{1,0:T(1,128)} %prior_ref.3), custom_call_target="tpu_custom_call" | custom-call | tf_op jit(solution)/shard_map/pallas_call | solution.py:210
  8.9 1.3 %collective-permute-start.7 = (f32[128,1408]{1,0:T(8,128)S(1)}, f32[128,1408]{1,0:T(8,128)S(1)}, u32[]{:S(2)}, u32[]{:S(2)}) collective-permute-start(f32[128,1408]{1,0:T(8,128)S(1)} %add_select_fusion), channel_id=1, source_target_pairs={{0,3},{1,4},{2,5},{3,6},{4,7},{5,8},{6,9},{7,10},{8,11},{9,12},{10... | collective-permute-start | bytes 2162696 | tf_op jit(solution)/shard_map/ppermute | solution.py:352
  10.3 1.3 %collective-permute-start.13 = (f32[128,1024]{1,0:T(8,128)S(1)}, f32[128,1024]{1,0:T(8,128)S(1)}, u32[]{:S(2)}, u32[]{:S(2)}) collective-permute-start(f32[128,1024]{1,0:T(8,128)S(1)} %add_select_fusion.1), channel_id=1, source_target_pairs={{0,3},{1,4},{2,5},{3,6},{4,7},{5,8},{6,9},{7,10},{8,11},{9,12},{10... | collective-permute-start | bytes 1572872 | tf_op jit(solution)/shard_map/ppermute | solution.py:352
  11.6 1.3 %collective-permute-start.10 = (f32[128,896]{1,0:T(8,128)S(1)}, f32[128,896]{1,0:T(8,128)S(1)}, u32[]{:S(2)}, u32[]{:S(2)}) collective-permute-start(f32[128,896]{1,0:T(8,128)S(1)} %add_select_fusion.2), channel_id=1, source_target_pairs={{0,3},{1,4},{2,5},{3,6},{4,7},{5,8},{6,9},{7,10},{8,11},{9,12},{10... | collective-permute-start | bytes 1376264 | tf_op jit(solution)/shard_map/ppermute | solution.py:352
  14.1 1.3 %collective-permute-start.1 = (f32[128,768]{1,0:T(8,128)S(1)}, f32[128,768]{1,0:T(8,128)S(1)}, u32[]{:S(2)}, u32[]{:S(2)}) collective-permute-start(f32[128,768]{1,0:T(8,128)S(1)} %add_select_fusion.3), channel_id=1, source_target_pairs={{0,3},{1,4},{2,5},{3,6},{4,7},{5,8},{6,9},{7,10},{8,11},{9,12},{10... | collective-permute-start | bytes 1179656 | tf_op jit(solution)/shard_map/ppermute | solution.py:352
  15.4 27.8 %collective-permute-done.13.refs_0_ = f32[128,1024]{1,0:T(8,128)S(1)} collective-permute-done((f32[128,1024]{1,0:T(8,128)S(1)}, f32[128,1024]{1,0:T(8,128)S(1)}, u32[]{:S(2)}, u32[]{:S(2)}) %collective-permute-start.13) | collective-permute-done | bytes 524320 | tf_op jit(solution)/shard_map/ppermute | solution.py:352
  43.2 1.3 %collective-permute-start.14 = (f32[128,1024]{1,0:T(8,128)S(1)}, f32[128,1024]{1,0:T(8,128)S(1)}, u32[]{:S(2)}, u32[]{:S(2)}) collective-permute-start(f32[128,1024]{1,0:T(8,128)S(1)} %collective-permute-done.13.refs_0_), channel_id=1, source_target_pairs={{1,0},{3,2},{5,4},{7,6},{9,8},{11,10},{13,12},{15,14},{17,16},{19,... | collective-permute-start | bytes 1572872 | tf_op jit(solution)/shard_map/ppermute | solution.py:353
  44.5 1.3 %collective-permute-start.8 = (f32[128,1408]{1,0:T(8,128)S(1)}, f32[128,1408]{1,0:T(8,128)S(1)}, u32[]{:S(2)}, u32[]{:S(2)}) collective-permute-start(f32[128,1408]{1,0:T(8,128)S(1)} %collective-permute-done.7.refs_0_), channel_id=1, source_target_pairs={{1,0},{3,2},{5,4},{7,6},{9,8},{11,10},{13,12},{15,14},{17,16},{19,... | collective-permute-start | bytes 2162696 | tf_op jit(solution)/shard_map/ppermute | solution.py:353
  46.9 1.3 %collective-permute-start.4 = (f32[128,512]{1,0:T(8,128)S(1)}, f32[128,512]{1,0:T(8,128)S(1)}, u32[]{:S(2)}, u32[]{:S(2)}) collective-permute-start(f32[128,512]{1,0:T(8,128)S(1)} %add_select_fusion.4), channel_id=1, source_target_pairs={{0,3},{1,4},{2,5},{3,6},{4,7},{5,8},{6,9},{7,10},{8,11},{9,12},{10... | collective-permute-start | bytes 786440 | tf_op jit(solution)/shard_map/ppermute | solution.py:352
  48.2 4.8 %collective-permute-done.10.refs_0_ = f32[128,896]{1,0:T(8,128)S(1)} collective-permute-done((f32[128,896]{1,0:T(8,128)S(1)}, f32[128,896]{1,0:T(8,128)S(1)}, u32[]{:S(2)}, u32[]{:S(2)}) %collective-permute-start.10) | collective-permute-done | bytes 458784 | tf_op jit(solution)/shard_map/ppermute | solution.py:352
  53.0 1.3 %collective-permute-start.11 = (f32[128,896]{1,0:T(8,128)S(1)}, f32[128,896]{1,0:T(8,128)S(1)}, u32[]{:S(2)}, u32[]{:S(2)}) collective-permute-start(f32[128,896]{1,0:T(8,128)S(1)} %collective-permute-done.10.refs_0_), channel_id=1, source_target_pairs={{1,0},{3,2},{5,4},{7,6},{9,8},{11,10},{13,12},{15,14},{17,16},{19,... | collective-permute-start | bytes 1376264 | tf_op jit(solution)/shard_map/ppermute | solution.py:353
  54.3 7.1 %collective-permute-done.1.refs_0_ = f32[128,768]{1,0:T(8,128)S(1)} collective-permute-done((f32[128,768]{1,0:T(8,128)S(1)}, f32[128,768]{1,0:T(8,128)S(1)}, u32[]{:S(2)}, u32[]{:S(2)}) %collective-permute-start.1) | collective-permute-done | bytes 393248 | tf_op jit(solution)/shard_map/ppermute | solution.py:352
  61.4 1.3 %collective-permute-start.2 = (f32[128,768]{1,0:T(8,128)S(1)}, f32[128,768]{1,0:T(8,128)S(1)}, u32[]{:S(2)}, u32[]{:S(2)}) collective-permute-start(f32[128,768]{1,0:T(8,128)S(1)} %collective-permute-done.1.refs_0_), channel_id=1, source_target_pairs={{1,0},{3,2},{5,4},{7,6},{9,8},{11,10},{13,12},{15,14},{17,16},{19,... | collective-permute-start | bytes 1179656 | tf_op jit(solution)/shard_map/ppermute | solution.py:353
  62.7 3.8 %collective-permute-done.4.refs_0_ = f32[128,512]{1,0:T(8,128)S(1)} collective-permute-done((f32[128,512]{1,0:T(8,128)S(1)}, f32[128,512]{1,0:T(8,128)S(1)}, u32[]{:S(2)}, u32[]{:S(2)}) %collective-permute-start.4) | collective-permute-done | bytes 262176 | tf_op jit(solution)/shard_map/ppermute | solution.py:352
  66.5 1.5 %collective-permute-start.5 = (f32[128,512]{1,0:T(8,128)S(1)}, f32[128,512]{1,0:T(8,128)S(1)}, u32[]{:S(2)}, u32[]{:S(2)}) collective-permute-start(f32[128,512]{1,0:T(8,128)S(1)} %collective-permute-done.4.refs_0_), channel_id=1, source_target_pairs={{1,0},{3,2},{5,4},{7,6},{9,8},{11,10},{13,12},{15,14},{17,16},{19,... | collective-permute-start | bytes 786440 | tf_op jit(solution)/shard_map/ppermute | solution.py:353
  68.0 3.7 %shard_map.39.refs_4_ = f32[1024,1024]{1,0:T(8,128)} custom-call(s32[1]{0:T(128)} %bitcast.odd_ref, f32[128,1024]{1,0:T(8,128)S(1)} %collective-permute-done.13.refs_0_, f32[128,1024]{1,0:T(8,128)S(1)} %collective-permute-done.14.refs_1_, f32[128,1024]{1,0:T(8,128)S(1)} %shard_map.38.refs_2_, f32[128,1024]{1,0:T(8,128)S(1)} %collective-permute-done.12.refs_3_), custom_call_target="tpu_custom_call" | custom-call | tf_op jit(solution)/shard_map/pallas_call | solution.py:326
  71.7 4.9 %shard_map.40.refs_6_.refs_5_ = f32[1024,1024]{1,0:T(8,128)} custom-call(s32[1]{0:T(128)} %bitcast.odd_ref, f32[128,896]{1,0:T(8,128)S(1)} %collective-permute-done.10.refs_0_, f32[128,896]{1,0:T(8,128)S(1)} %collective-permute-done.11.refs_1_, f32[128,896]{1,0:T(8,128)S(1)} %get-tuple-element.20.refs_2_, ...), custom_call_target="tpu_custom_call", output_to_operand_aliasing={{}: (5, {})} | custom-call | tf_op jit(solution)/shard_map/pallas_call | solution.py:326
  76.7 2.2 %copy-done = f32[1024,1024]{1,0:T(8,128)S(1)} copy-done((f32[1024,1024]{1,0:T(8,128)S(1)}, f32[1024,1024]{1,0:T(8,128)}, u32[]{:S(2)}) %copy-start) | copy-done | bytes 4194328
  78.9 2.8 %settle.1 = (f32[128,1408]{1,0:T(8,128)S(1)}, f32[128,512]{1,0:T(8,128)S(1)}, f32[128,768]{1,0:T(8,128)S(1)}) custom-call(s32[1]{0:T(128)} %bitcast.odd_ref, f32[128,1408]{1,0:T(8,128)S(1)} %get-tuple-element.19.refs_0_, f32[128,512]{1,0:T(8,128)} %get-tuple-element.18.refs_1_, f32[128,768]{1,0:T(8,128)} %get-tuple-element.17.refs_2_, ...), custom_call_target="tpu_custom_call" | custom-call | tf_op jit(solution)/shard_map/settle/pallas_call | solution.py:242
  81.7 6.5 %shard_map.41 = (f32[1024,1024]{1,0:T(8,128)}, f32[128,512]{1,0:T(8,128)S(1)}, f32[128,768]{1,0:T(8,128)S(1)}) custom-call(s32[1]{0:T(128)} %bitcast.odd_ref, f32[128,1408]{1,0:T(8,128)S(1)} %collective-permute-done.7.refs_0_, f32[128,1408]{1,0:T(8,128)S(1)} %collective-permute-done.8.refs_1_, ...), custom_call_target="tpu_custom_call", output_to_operand_aliasing={{0}: (6, {})} | custom-call | tf_op jit(solution)/shard_map/pallas_call | solution.py:326
  88.3 3.5 %shard_map.42 = (f32[1024,1024]{1,0:T(8,128)}, f32[128,768]{1,0:T(8,128)S(1)}) custom-call(s32[1]{0:T(128)} %bitcast.odd_ref, f32[128,512]{1,0:T(8,128)S(1)} %collective-permute-done.4.refs_0_, f32[128,512]{1,0:T(8,128)S(1)} %collective-permute-done.5.refs_1_, f32[128,512]{1,0:T(8,128)S(1)} %get-tuple-element.24.refs_2_, ...), custom_call_target="tpu_custom_call", output_to_operand_aliasing={{0}: (5, {})} | custom-call | tf_op jit(solution)/shard_map/pallas_call | solution.py:326
  91.9 9.3 %shard_map.43 = f32[1024,1024]{1,0:T(8,128)} custom-call(s32[1]{0:T(128)} %bitcast.odd_ref, f32[128,768]{1,0:T(8,128)S(1)} %collective-permute-done.1.refs_0_, f32[128,768]{1,0:T(8,128)S(1)} %collective-permute-done.2.refs_1_, f32[128,768]{1,0:T(8,128)S(1)} %get-tuple-element.27.refs_2_, ...), custom_call_target="tpu_custom_call", output_to_operand_aliasing={{}: (4, {})} | custom-call | tf_op jit(solution)/shard_map/pallas_call | solution.py:326
  (25 shorter events, 4.9 us)
Async XLA Ops:
  0.7 2.2 %copy-start.1 = (bf16[2048,1024]{1,0:T(8,128)(2,1)S(1)}, bf16[2048,1024]{1,0:T(8,128)(2,1)}, u32[]{:S(2)}) copy-start(bf16[2048,1024]{1,0:T(8,128)(2,1)} %h_ref.3) | copy-start | bytes 12582916
  2.8 0.7 copy-start.2
  5.4 3.4 %collective-permute-start.6 = (f32[128,1408]{1,0:T(8,128)S(1)}, f32[128,1408]{1,0:T(8,128)S(1)}, u32[]{:S(2)}, u32[]{:S(2)}) collective-permute-start(f32[128,1408]{1,0:T(8,128)S(1)} %get-tuple-element.19.refs_0_), channel_id=1, source_target_pairs={{0,1},{1,0},{2,3},{3,2},{4,5},{5,4},{6,7},{7,6},{8,9},{9,8},{10,11... | collective-permute-start | bytes 2162696 | tf_op jit(solution)/shard_map/ppermute | solution.py:350
  7.7 2.5 %collective-permute-start.12 = (f32[128,1024]{1,0:T(8,128)S(1)}, f32[128,1024]{1,0:T(8,128)S(1)}, u32[]{:S(2)}, u32[]{:S(2)}) collective-permute-start(f32[128,1024]{1,0:T(8,128)S(1)} %shard_map.38.refs_2_), channel_id=1, source_target_pairs={{0,1},{1,0},{2,3},{3,2},{4,5},{5,4},{6,7},{7,6},{8,9},{9,8},{10,11... | collective-permute-start | bytes 1572872 | tf_op jit(solution)/shard_map/ppermute | solution.py:350
  7.8 3.8 %collective-permute-start.9 = (f32[128,896]{1,0:T(8,128)S(1)}, f32[128,896]{1,0:T(8,128)S(1)}, u32[]{:S(2)}, u32[]{:S(2)}) collective-permute-start(f32[128,896]{1,0:T(8,128)S(1)} %get-tuple-element.20.refs_2_), channel_id=1, source_target_pairs={{0,1},{1,0},{2,3},{3,2},{4,5},{5,4},{6,7},{7,6},{8,9},{9,8},{10,11... | collective-permute-start | bytes 1376264 | tf_op jit(solution)/shard_map/ppermute | solution.py:350
  8.3 4.6 %collective-permute-start = (f32[128,768]{1,0:T(8,128)}, f32[128,768]{1,0:T(8,128)}, u32[]{:S(2)}, u32[]{:S(2)}) collective-permute-start(f32[128,768]{1,0:T(8,128)} %get-tuple-element.17.refs_2_), channel_id=1, source_target_pairs={{0,1},{1,0},{2,3},{3,2},{4,5},{5,4},{6,7},{7,6},{8,9},{9,8},{10,11... | collective-permute-start | bytes 1179656 | tf_op jit(solution)/shard_map/ppermute | solution.py:350
  8.4 37.5 %collective-permute-start.3 = (f32[128,512]{1,0:T(8,128)}, f32[128,512]{1,0:T(8,128)}, u32[]{:S(2)}, u32[]{:S(2)}) collective-permute-start(f32[128,512]{1,0:T(8,128)} %get-tuple-element.18.refs_1_), channel_id=1, source_target_pairs={{0,1},{1,0},{2,3},{3,2},{4,5},{5,4},{6,7},{7,6},{8,9},{9,8},{10,11... | collective-permute-start | bytes 786440 | tf_op jit(solution)/shard_map/ppermute | solution.py:350
  8.9 35.6 %collective-permute-start.7 = (f32[128,1408]{1,0:T(8,128)S(1)}, f32[128,1408]{1,0:T(8,128)S(1)}, u32[]{:S(2)}, u32[]{:S(2)}) collective-permute-start(f32[128,1408]{1,0:T(8,128)S(1)} %add_select_fusion), channel_id=1, source_target_pairs={{0,3},{1,4},{2,5},{3,6},{4,7},{5,8},{6,9},{7,10},{8,11},{9,12},{10... | collective-permute-start | bytes 2162696 | tf_op jit(solution)/shard_map/ppermute | solution.py:352
  10.3 32.9 %collective-permute-start.13 = (f32[128,1024]{1,0:T(8,128)S(1)}, f32[128,1024]{1,0:T(8,128)S(1)}, u32[]{:S(2)}, u32[]{:S(2)}) collective-permute-start(f32[128,1024]{1,0:T(8,128)S(1)} %add_select_fusion.1), channel_id=1, source_target_pairs={{0,3},{1,4},{2,5},{3,6},{4,7},{5,8},{6,9},{7,10},{8,11},{9,12},{10... | collective-permute-start | bytes 1572872 | tf_op jit(solution)/shard_map/ppermute | solution.py:352
  11.6 41.4 %collective-permute-start.10 = (f32[128,896]{1,0:T(8,128)S(1)}, f32[128,896]{1,0:T(8,128)S(1)}, u32[]{:S(2)}, u32[]{:S(2)}) collective-permute-start(f32[128,896]{1,0:T(8,128)S(1)} %add_select_fusion.2), channel_id=1, source_target_pairs={{0,3},{1,4},{2,5},{3,6},{4,7},{5,8},{6,9},{7,10},{8,11},{9,12},{10... | collective-permute-start | bytes 1376264 | tf_op jit(solution)/shard_map/ppermute | solution.py:352
  14.1 47.3 %collective-permute-start.1 = (f32[128,768]{1,0:T(8,128)S(1)}, f32[128,768]{1,0:T(8,128)S(1)}, u32[]{:S(2)}, u32[]{:S(2)}) collective-permute-start(f32[128,768]{1,0:T(8,128)S(1)} %add_select_fusion.3), channel_id=1, source_target_pairs={{0,3},{1,4},{2,5},{3,6},{4,7},{5,8},{6,9},{7,10},{8,11},{9,12},{10... | collective-permute-start | bytes 1179656 | tf_op jit(solution)/shard_map/ppermute | solution.py:352
  43.2 24.8 %collective-permute-start.14 = (f32[128,1024]{1,0:T(8,128)S(1)}, f32[128,1024]{1,0:T(8,128)S(1)}, u32[]{:S(2)}, u32[]{:S(2)}) collective-permute-start(f32[128,1024]{1,0:T(8,128)S(1)} %collective-permute-done.13.refs_0_), channel_id=1, source_target_pairs={{1,0},{3,2},{5,4},{7,6},{9,8},{11,10},{13,12},{15,14},{17,16},{19,... | collective-permute-start | bytes 1572872 | tf_op jit(solution)/shard_map/ppermute | solution.py:353
  44.5 37.2 %collective-permute-start.8 = (f32[128,1408]{1,0:T(8,128)S(1)}, f32[128,1408]{1,0:T(8,128)S(1)}, u32[]{:S(2)}, u32[]{:S(2)}) collective-permute-start(f32[128,1408]{1,0:T(8,128)S(1)} %collective-permute-done.7.refs_0_), channel_id=1, source_target_pairs={{1,0},{3,2},{5,4},{7,6},{9,8},{11,10},{13,12},{15,14},{17,16},{19,... | collective-permute-start | bytes 2162696 | tf_op jit(solution)/shard_map/ppermute | solution.py:353
  46.9 19.6 %collective-permute-start.4 = (f32[128,512]{1,0:T(8,128)S(1)}, f32[128,512]{1,0:T(8,128)S(1)}, u32[]{:S(2)}, u32[]{:S(2)}) collective-permute-start(f32[128,512]{1,0:T(8,128)S(1)} %add_select_fusion.4), channel_id=1, source_target_pairs={{0,3},{1,4},{2,5},{3,6},{4,7},{5,8},{6,9},{7,10},{8,11},{9,12},{10... | collective-permute-start | bytes 786440 | tf_op jit(solution)/shard_map/ppermute | solution.py:352
  53.0 18.7 %collective-permute-start.11 = (f32[128,896]{1,0:T(8,128)S(1)}, f32[128,896]{1,0:T(8,128)S(1)}, u32[]{:S(2)}, u32[]{:S(2)}) collective-permute-start(f32[128,896]{1,0:T(8,128)S(1)} %collective-permute-done.10.refs_0_), channel_id=1, source_target_pairs={{1,0},{3,2},{5,4},{7,6},{9,8},{11,10},{13,12},{15,14},{17,16},{19,... | collective-permute-start | bytes 1376264 | tf_op jit(solution)/shard_map/ppermute | solution.py:353
  61.4 30.4 %collective-permute-start.2 = (f32[128,768]{1,0:T(8,128)S(1)}, f32[128,768]{1,0:T(8,128)S(1)}, u32[]{:S(2)}, u32[]{:S(2)}) collective-permute-start(f32[128,768]{1,0:T(8,128)S(1)} %collective-permute-done.1.refs_0_), channel_id=1, source_target_pairs={{1,0},{3,2},{5,4},{7,6},{9,8},{11,10},{13,12},{15,14},{17,16},{19,... | collective-permute-start | bytes 1179656 | tf_op jit(solution)/shard_map/ppermute | solution.py:353
  66.5 21.7 %collective-permute-start.5 = (f32[128,512]{1,0:T(8,128)S(1)}, f32[128,512]{1,0:T(8,128)S(1)}, u32[]{:S(2)}, u32[]{:S(2)}) collective-permute-start(f32[128,512]{1,0:T(8,128)S(1)} %collective-permute-done.4.refs_0_), channel_id=1, source_target_pairs={{1,0},{3,2},{5,4},{7,6},{9,8},{11,10},{13,12},{15,14},{17,16},{19,... | collective-permute-start | bytes 786440 | tf_op jit(solution)/shard_map/ppermute | solution.py:353
  76.7 2.2 %copy-start = (f32[1024,1024]{1,0:T(8,128)S(1)}, f32[1024,1024]{1,0:T(8,128)}, u32[]{:S(2)}) copy-start(f32[1024,1024]{1,0:T(8,128)} %shard_map.40.refs_6_.refs_5_) | copy-start | bytes 12582916

commit v6 on v5

--- a/solution.py
+++ b/solution.py
@@ -13,7 +13,7 @@
 LEAD = 3
 DEPTH = 512
 ROOM = 24 << 20
-CUTS = (1, 2, 4, 5)
+CUTS = (1, 2, 4, 6)
 SETTLE = 2
 
 
@@ -239,10 +239,11 @@
 def settle_rows(groups, size, odd, owns, pairs, factor):
     vmem, smem, f32 = pl.BlockSpec(memory_space=pltpu.VMEM), pl.BlockSpec(memory_space=pltpu.SMEM), jnp.float32
     known = groups[0][0] * LANES
+    factor = pltpu.with_memory_space_constraint(factor, pltpu.HBM)
     return pl.pallas_call(
         functools.partial(settle_kernel, groups),
         out_shape=[jax.ShapeDtypeStruct(own.shape, f32) for own in owns],
-        in_specs=[smem] + [vmem] * (2 * len(groups)) + [pl.BlockSpec(memory_space=pl.ANY)],
+        in_specs=[smem] + [vmem] * (2 * len(groups)) + [pl.BlockSpec(memory_space=pltpu.HBM)],
         out_specs=[vmem] * len(groups),
         scratch_shapes=[pltpu.VMEM((known, size - known), f32), pltpu.SemaphoreType.DMA],
         compiler_params=pltpu.CompilerParams(vmem_limit_bytes=ROOM),

time: 102 us -> 109 us (1.069)
  waiting for transfers between devices: 43.5 us -> 47.4 us
  starting transfers between devices: 14.9 us -> 18.7 us
  local copies, waits for them, and re-layouts: 5.05 us -> 3.54 us
    ppermute x5, starting transfers between devices: 1.75 us -> 5.54 us  [body(): pair = lax.ppermute(own, 'tm', swap)]
    ppermute x5, waiting for transfers between devices: 43.4 us -> 47.1 us  [body(): far = lax.ppermute(send, 'tm', ahead)]
    unnamed x6 -> x8, local copies, waits for them, and re-layouts: 5.05 us -> 3.54 us
    pallas_call x5, Pallas kernels: 28 us -> 29.1 us  [factor_rows(): pl.pallas_call(functools.partial(factor_kernel, group, later, known, len(...]
  transfers between devices with their start and end apart: 15 -> 15, of which waited for: 4 -> 4; matrix products, arithmetic and copies ran while one was open for 2% -> 2% of each run, Pallas kernels for 23% -> 26%
where the time goes in v6:
time: 109 us; the launch traced here: 108 us
  waiting for transfers between devices  47.4 us (43%)
  Pallas kernels  35.3 us (32%)
  starting transfers between devices  18.7 us (17%)
  local copies, waits for them, and re-layouts  3.54 us (3%)
  other arithmetic  2.31 us (2%)
  between operations  1.11 us (1%)
    ppermute x5, waiting for transfers between devices, body(): far = lax.ppermute(send, 'tm', ahead)  47.1 us
    pallas_call x5, Pallas kernels, factor_rows(): pl.pallas_call(functools.partial(factor_kernel, group, later, known, len(...  29.1 us
    ppermute x5, starting transfers between devices, body(): near = lax.ppermute(far, 'tm', inward)  6.74 us
    ppermute x5, starting transfers between devices, body(): far = lax.ppermute(send, 'tm', ahead)  6.46 us
    ppermute x5, starting transfers between devices, body(): pair = lax.ppermute(own, 'tm', swap)  5.54 us
    pallas_call x1, Pallas kernels, settle_rows(): pl.pallas_call(functools.partial(settle_kernel, groups), out_shape=[jax.S...  3.65 us
    unnamed x8, local copies, waits for them, and re-layouts  3.54 us
    pallas_call x2, Pallas kernels, gram_rows(): pl.pallas_call(functools.partial(gram_kernel, groups, fetched), out_shape...  2.58 us
  transfers between devices with their start and end apart: 15, of which 4 were waited for; matrix products, arithmetic and copies ran while one was open for 2% of the time, Pallas kernels for 26%

profile of v6, /device:TPU:25, one launch (start us, length us, event | category | flops | bytes accessed | tf_op | source)
XLA Modules:
  0.0 108.5 jit_solution(13723642121689369742)
XLA Ops:
  0.7 2.2 %copy-done = bf16[2048,1024]{1,0:T(8,128)(2,1)S(1)} copy-done((bf16[2048,1024]{1,0:T(8,128)(2,1)S(1)}, bf16[2048,1024]{1,0:T(8,128)(2,1)}, u32[]{:S(2)}) %copy-start) | copy-done | bytes 4194328
  5.8 1.7 %shard_map.38.refs_2_ = f32[128,1024]{1,0:T(8,128)S(1)} custom-call(s32[1]{0:T(128)S(6)} %copy.12.count_ref, bf16[2048,1024]{1,0:T(8,128)(2,1)} %h_ref.3, f32[1,1024]{1,0:T(1,128)} %prior_ref.3), custom_call_target="tpu_custom_call" | custom-call | tf_op jit(solution)/shard_map/pallas_call | solution.py:210
  8.4 1.1 add_select_fusion.2
  9.5 1.3 %collective-permute-start.10 = (f32[128,896]{1,0:T(8,128)S(1)}, f32[128,896]{1,0:T(8,128)S(1)}, u32[]{:S(2)}, u32[]{:S(2)}) collective-permute-start(f32[128,896]{1,0:T(8,128)S(1)} %add_select_fusion.2), channel_id=1, source_target_pairs={{0,3},{1,4},{2,5},{3,6},{4,7},{5,8},{6,9},{7,10},{8,11},{9,12},{10... | collective-permute-start | bytes 1376264 | tf_op jit(solution)/shard_map/ppermute | solution.py:353
  10.9 1.3 %collective-permute-start.7 = (f32[128,1408]{1,0:T(8,128)S(1)}, f32[128,1408]{1,0:T(8,128)S(1)}, u32[]{:S(2)}, u32[]{:S(2)}) collective-permute-start(f32[128,1408]{1,0:T(8,128)S(1)} %add_select_fusion), channel_id=1, source_target_pairs={{0,3},{1,4},{2,5},{3,6},{4,7},{5,8},{6,9},{7,10},{8,11},{9,12},{10... | collective-permute-start | bytes 2162696 | tf_op jit(solution)/shard_map/ppermute | solution.py:353
  12.3 1.3 %collective-permute-start.13 = (f32[128,1024]{1,0:T(8,128)S(1)}, f32[128,1024]{1,0:T(8,128)S(1)}, u32[]{:S(2)}, u32[]{:S(2)}) collective-permute-start(f32[128,1024]{1,0:T(8,128)S(1)} %add_select_fusion.1), channel_id=1, source_target_pairs={{0,3},{1,4},{2,5},{3,6},{4,7},{5,8},{6,9},{7,10},{8,11},{9,12},{10... | collective-permute-start | bytes 1572872 | tf_op jit(solution)/shard_map/ppermute | solution.py:353
  13.6 1.1 add_select_fusion.3
  14.6 1.3 %collective-permute-start.4 = (f32[128,896]{1,0:T(8,128)S(1)}, f32[128,896]{1,0:T(8,128)S(1)}, u32[]{:S(2)}, u32[]{:S(2)}) collective-permute-start(f32[128,896]{1,0:T(8,128)S(1)} %add_select_fusion.3), channel_id=1, source_target_pairs={{0,3},{1,4},{2,5},{3,6},{4,7},{5,8},{6,9},{7,10},{8,11},{9,12},{10... | collective-permute-start | bytes 1376264 | tf_op jit(solution)/shard_map/ppermute | solution.py:353
  16.0 4.2 %collective-permute-start = (f32[128,384]{1,0:T(8,128)S(1)}, f32[128,384]{1,0:T(8,128)S(1)}, u32[]{:S(2)}, u32[]{:S(2)}) collective-permute-start(f32[128,384]{1,0:T(8,128)S(1)} %copy-done.2), channel_id=1, source_target_pairs={{0,1},{1,0},{2,3},{3,2},{4,5},{5,4},{6,7},{7,6},{8,9},{9,8},{10,11... | collective-permute-start | bytes 589832 | tf_op jit(solution)/shard_map/ppermute | solution.py:351
  20.2 22.2 %collective-permute-done.7.refs_0_ = f32[128,1408]{1,0:T(8,128)S(1)} collective-permute-done((f32[128,1408]{1,0:T(8,128)S(1)}, f32[128,1408]{1,0:T(8,128)S(1)}, u32[]{:S(2)}, u32[]{:S(2)}) %collective-permute-start.7) | collective-permute-done | bytes 720928 | tf_op jit(solution)/shard_map/ppermute | solution.py:353
  42.4 1.3 %collective-permute-start.8 = (f32[128,1408]{1,0:T(8,128)S(1)}, f32[128,1408]{1,0:T(8,128)S(1)}, u32[]{:S(2)}, u32[]{:S(2)}) collective-permute-start(f32[128,1408]{1,0:T(8,128)S(1)} %collective-permute-done.7.refs_0_), channel_id=1, source_target_pairs={{1,0},{3,2},{5,4},{7,6},{9,8},{11,10},{13,12},{15,14},{17,16},{19,... | collective-permute-start | bytes 2162696 | tf_op jit(solution)/shard_map/ppermute | solution.py:354
  43.7 1.3 %collective-permute-start.11 = (f32[128,896]{1,0:T(8,128)S(1)}, f32[128,896]{1,0:T(8,128)S(1)}, u32[]{:S(2)}, u32[]{:S(2)}) collective-permute-start(f32[128,896]{1,0:T(8,128)S(1)} %collective-permute-done.10.refs_0_), channel_id=1, source_target_pairs={{1,0},{3,2},{5,4},{7,6},{9,8},{11,10},{13,12},{15,14},{17,16},{19,... | collective-permute-start | bytes 1376264 | tf_op jit(solution)/shard_map/ppermute | solution.py:354
  45.0 17.8 %collective-permute-done.4.refs_0_ = f32[128,896]{1,0:T(8,128)S(1)} collective-permute-done((f32[128,896]{1,0:T(8,128)S(1)}, f32[128,896]{1,0:T(8,128)S(1)}, u32[]{:S(2)}, u32[]{:S(2)}) %collective-permute-start.4) | collective-permute-done | bytes 458784 | tf_op jit(solution)/shard_map/ppermute | solution.py:353
  62.8 1.3 %collective-permute-start.5 = (f32[128,896]{1,0:T(8,128)S(1)}, f32[128,896]{1,0:T(8,128)S(1)}, u32[]{:S(2)}, u32[]{:S(2)}) collective-permute-start(f32[128,896]{1,0:T(8,128)S(1)} %collective-permute-done.4.refs_0_), channel_id=1, source_target_pairs={{1,0},{3,2},{5,4},{7,6},{9,8},{11,10},{13,12},{15,14},{17,16},{19,... | collective-permute-start | bytes 1376264 | tf_op jit(solution)/shard_map/ppermute | solution.py:354
  64.2 1.3 %collective-permute-start.14 = (f32[128,1024]{1,0:T(8,128)S(1)}, f32[128,1024]{1,0:T(8,128)S(1)}, u32[]{:S(2)}, u32[]{:S(2)}) collective-permute-start(f32[128,1024]{1,0:T(8,128)S(1)} %collective-permute-done.13.refs_0_), channel_id=1, source_target_pairs={{1,0},{3,2},{5,4},{7,6},{9,8},{11,10},{13,12},{15,14},{17,16},{19,... | collective-permute-start | bytes 1572872 | tf_op jit(solution)/shard_map/ppermute | solution.py:354
  65.5 1.3 %collective-permute-start.1 = (f32[128,384]{1,0:T(8,128)S(1)}, f32[128,384]{1,0:T(8,128)S(1)}, u32[]{:S(2)}, u32[]{:S(2)}) collective-permute-start(f32[128,384]{1,0:T(8,128)S(1)} %add_select_fusion.4), channel_id=1, source_target_pairs={{0,3},{1,4},{2,5},{3,6},{4,7},{5,8},{6,9},{7,10},{8,11},{9,12},{10... | collective-permute-start | bytes 589832 | tf_op jit(solution)/shard_map/ppermute | solution.py:353
  66.8 7.1 %collective-permute-done.1.refs_0_ = f32[128,384]{1,0:T(8,128)S(1)} collective-permute-done((f32[128,384]{1,0:T(8,128)S(1)}, f32[128,384]{1,0:T(8,128)S(1)}, u32[]{:S(2)}, u32[]{:S(2)}) %collective-permute-start.1) | collective-permute-done | bytes 196640 | tf_op jit(solution)/shard_map/ppermute | solution.py:353
  74.0 1.5 %collective-permute-start.2 = (f32[128,384]{1,0:T(8,128)S(1)}, f32[128,384]{1,0:T(8,128)S(1)}, u32[]{:S(2)}, u32[]{:S(2)}) collective-permute-start(f32[128,384]{1,0:T(8,128)S(1)} %collective-permute-done.1.refs_0_), channel_id=1, source_target_pairs={{1,0},{3,2},{5,4},{7,6},{9,8},{11,10},{13,12},{15,14},{17,16},{19,... | collective-permute-start | bytes 589832 | tf_op jit(solution)/shard_map/ppermute | solution.py:354
  75.5 3.7 %shard_map.39.refs_4_ = f32[1024,1024]{1,0:T(8,128)} custom-call(s32[1]{0:T(128)} %bitcast.odd_ref, f32[128,1024]{1,0:T(8,128)S(1)} %collective-permute-done.13.refs_0_, f32[128,1024]{1,0:T(8,128)S(1)} %collective-permute-done.14.refs_1_, f32[128,1024]{1,0:T(8,128)S(1)} %shard_map.38.refs_2_, f32[128,1024]{1,0:T(8,128)S(1)} %collective-permute-done.12.refs_3_), custom_call_target="tpu_custom_call" | custom-call | tf_op jit(solution)/shard_map/pallas_call | solution.py:327
  79.2 6.1 %shard_map.40.refs_6_.refs_5_ = f32[1024,1024]{1,0:T(8,128)} custom-call(s32[1]{0:T(128)} %bitcast.odd_ref, f32[128,896]{1,0:T(8,128)S(1)} %collective-permute-done.10.refs_0_, f32[128,896]{1,0:T(8,128)S(1)} %collective-permute-done.11.refs_1_, f32[128,896]{1,0:T(8,128)S(1)} %get-tuple-element.20.refs_2_, ...), custom_call_target="tpu_custom_call", output_to_operand_aliasing={{}: (5, {})} | custom-call | tf_op jit(solution)/shard_map/pallas_call | solution.py:327
  85.3 3.6 %settle.1 = (f32[128,1408]{1,0:T(8,128)S(1)}, f32[128,896]{1,0:T(8,128)S(1)}, f32[128,384]{1,0:T(8,128)S(1)}) custom-call(s32[1]{0:T(128)} %bitcast.odd_ref, f32[128,1408]{1,0:T(8,128)S(1)} %get-tuple-element.19.refs_0_, f32[128,896]{1,0:T(8,128)S(1)} %get-tuple-element.18.refs_1_, f32[128,384]{1,0:T(8,128)S(1)} %copy-done.2, ...), custom_call_target="tpu_custom_call" | custom-call | tf_op jit(solution)/shard_map/settle/pallas_call | solution.py:243
  88.9 6.5 %shard_map.41 = (f32[1024,1024]{1,0:T(8,128)}, f32[128,896]{1,0:T(8,128)S(1)}, f32[128,384]{1,0:T(8,128)S(1)}) custom-call(s32[1]{0:T(128)} %bitcast.odd_ref, f32[128,1408]{1,0:T(8,128)S(1)} %collective-permute-done.7.refs_0_, f32[128,1408]{1,0:T(8,128)S(1)} %collective-permute-done.8.refs_1_, ...), custom_call_target="tpu_custom_call", output_to_operand_aliasing={{0}: (6, {})} | custom-call | tf_op jit(solution)/shard_map/pallas_call | solution.py:327
  95.5 6.7 %shard_map.42 = (f32[1024,1024]{1,0:T(8,128)}, f32[128,384]{1,0:T(8,128)S(1)}) custom-call(s32[1]{0:T(128)} %bitcast.odd_ref, f32[128,896]{1,0:T(8,128)S(1)} %collective-permute-done.4.refs_0_, f32[128,896]{1,0:T(8,128)S(1)} %collective-permute-done.5.refs_1_, f32[128,896]{1,0:T(8,128)S(1)} %get-tuple-element.24.refs_2_, ...), custom_call_target="tpu_custom_call", output_to_operand_aliasing={{0}: (5, {})} | custom-call | tf_op jit(solution)/shard_map/pallas_call | solution.py:327
  102.2 6.1 %shard_map.43 = f32[1024,1024]{1,0:T(8,128)} custom-call(s32[1]{0:T(128)} %bitcast.odd_ref, f32[128,384]{1,0:T(8,128)S(1)} %collective-permute-done.1.refs_0_, f32[128,384]{1,0:T(8,128)S(1)} %collective-permute-done.2.refs_1_, f32[128,384]{1,0:T(8,128)S(1)} %get-tuple-element.27.refs_2_, ...), custom_call_target="tpu_custom_call", output_to_operand_aliasing={{}: (4, {})} | custom-call | tf_op jit(solution)/shard_map/pallas_call | solution.py:327
  (27 shorter events, 4.1 us)
Async XLA Ops:
  0.7 2.2 %copy-start = (bf16[2048,1024]{1,0:T(8,128)(2,1)S(1)}, bf16[2048,1024]{1,0:T(8,128)(2,1)}, u32[]{:S(2)}) copy-start(bf16[2048,1024]{1,0:T(8,128)(2,1)} %h_ref.3) | copy-start | bytes 12582916
  2.8 0.7 copy-start.3
  4.4 0.7 copy-start.1
  5.1 5.7 %collective-permute-start.6 = (f32[128,1408]{1,0:T(8,128)S(1)}, f32[128,1408]{1,0:T(8,128)S(1)}, u32[]{:S(2)}, u32[]{:S(2)}) collective-permute-start(f32[128,1408]{1,0:T(8,128)S(1)} %get-tuple-element.19.refs_0_), channel_id=1, source_target_pairs={{0,1},{1,0},{2,3},{3,2},{4,5},{5,4},{6,7},{7,6},{8,9},{9,8},{10,11... | collective-permute-start | bytes 2162696 | tf_op jit(solution)/shard_map/ppermute | solution.py:351
  5.8 2.6 %collective-permute-start.9 = (f32[128,896]{1,0:T(8,128)S(1)}, f32[128,896]{1,0:T(8,128)}, u32[]{:S(2)}, u32[]{:S(2)}) collective-permute-start(f32[128,896]{1,0:T(8,128)S(1)} %get-tuple-element.20.refs_2_), channel_id=1, source_target_pairs={{0,1},{1,0},{2,3},{3,2},{4,5},{5,4},{6,7},{7,6},{8,9},{9,8},{10,11... | collective-permute-start | bytes 1376264 | tf_op jit(solution)/shard_map/ppermute | solution.py:351
  7.5 4.7 %collective-permute-start.12 = (f32[128,1024]{1,0:T(8,128)S(1)}, f32[128,1024]{1,0:T(8,128)S(1)}, u32[]{:S(2)}, u32[]{:S(2)}) collective-permute-start(f32[128,1024]{1,0:T(8,128)S(1)} %shard_map.38.refs_2_), channel_id=1, source_target_pairs={{0,1},{1,0},{2,3},{3,2},{4,5},{5,4},{6,7},{7,6},{8,9},{9,8},{10,11... | collective-permute-start | bytes 1572872 | tf_op jit(solution)/shard_map/ppermute | solution.py:351
  8.1 5.5 %collective-permute-start.3 = (f32[128,896]{1,0:T(8,128)S(1)}, f32[128,896]{1,0:T(8,128)}, u32[]{:S(2)}, u32[]{:S(2)}) collective-permute-start(f32[128,896]{1,0:T(8,128)S(1)} %get-tuple-element.18.refs_1_), channel_id=1, source_target_pairs={{0,1},{1,0},{2,3},{3,2},{4,5},{5,4},{6,7},{7,6},{8,9},{9,8},{10,11... | collective-permute-start | bytes 1376264 | tf_op jit(solution)/shard_map/ppermute | solution.py:351
  8.1 7.8 %copy-start.2 = (f32[128,384]{1,0:T(8,128)S(1)}, f32[128,384]{1,0:T(8,128)}, u32[]{:S(2)}) copy-start(f32[128,384]{1,0:T(8,128)} %copy-done.1) | copy-start | bytes 589828
  9.5 34.2 %collective-permute-start.10 = (f32[128,896]{1,0:T(8,128)S(1)}, f32[128,896]{1,0:T(8,128)S(1)}, u32[]{:S(2)}, u32[]{:S(2)}) collective-permute-start(f32[128,896]{1,0:T(8,128)S(1)} %add_select_fusion.2), channel_id=1, source_target_pairs={{0,3},{1,4},{2,5},{3,6},{4,7},{5,8},{6,9},{7,10},{8,11},{9,12},{10... | collective-permute-start | bytes 1376264 | tf_op jit(solution)/shard_map/ppermute | solution.py:353
  10.9 31.5 %collective-permute-start.7 = (f32[128,1408]{1,0:T(8,128)S(1)}, f32[128,1408]{1,0:T(8,128)S(1)}, u32[]{:S(2)}, u32[]{:S(2)}) collective-permute-start(f32[128,1408]{1,0:T(8,128)S(1)} %add_select_fusion), channel_id=1, source_target_pairs={{0,3},{1,4},{2,5},{3,6},{4,7},{5,8},{6,9},{7,10},{8,11},{9,12},{10... | collective-permute-start | bytes 2162696 | tf_op jit(solution)/shard_map/ppermute | solution.py:353
  12.3 51.9 %collective-permute-start.13 = (f32[128,1024]{1,0:T(8,128)S(1)}, f32[128,1024]{1,0:T(8,128)S(1)}, u32[]{:S(2)}, u32[]{:S(2)}) collective-permute-start(f32[128,1024]{1,0:T(8,128)S(1)} %add_select_fusion.1), channel_id=1, source_target_pairs={{0,3},{1,4},{2,5},{3,6},{4,7},{5,8},{6,9},{7,10},{8,11},{9,12},{10... | collective-permute-start | bytes 1572872 | tf_op jit(solution)/shard_map/ppermute | solution.py:353
  14.6 48.2 %collective-permute-start.4 = (f32[128,896]{1,0:T(8,128)S(1)}, f32[128,896]{1,0:T(8,128)S(1)}, u32[]{:S(2)}, u32[]{:S(2)}) collective-permute-start(f32[128,896]{1,0:T(8,128)S(1)} %add_select_fusion.3), channel_id=1, source_target_pairs={{0,3},{1,4},{2,5},{3,6},{4,7},{5,8},{6,9},{7,10},{8,11},{9,12},{10... | collective-permute-start | bytes 1376264 | tf_op jit(solution)/shard_map/ppermute | solution.py:353
  16.0 49.5 %collective-permute-start = (f32[128,384]{1,0:T(8,128)S(1)}, f32[128,384]{1,0:T(8,128)S(1)}, u32[]{:S(2)}, u32[]{:S(2)}) collective-permute-start(f32[128,384]{1,0:T(8,128)S(1)} %copy-done.2), channel_id=1, source_target_pairs={{0,1},{1,0},{2,3},{3,2},{4,5},{5,4},{6,7},{7,6},{8,9},{9,8},{10,11... | collective-permute-start | bytes 589832 | tf_op jit(solution)/shard_map/ppermute | solution.py:351
  42.4 46.6 %collective-permute-start.8 = (f32[128,1408]{1,0:T(8,128)S(1)}, f32[128,1408]{1,0:T(8,128)S(1)}, u32[]{:S(2)}, u32[]{:S(2)}) collective-permute-start(f32[128,1408]{1,0:T(8,128)S(1)} %collective-permute-done.7.refs_0_), channel_id=1, source_target_pairs={{1,0},{3,2},{5,4},{7,6},{9,8},{11,10},{13,12},{15,14},{17,16},{19,... | collective-permute-start | bytes 2162696 | tf_op jit(solution)/shard_map/ppermute | solution.py:354
  43.7 35.5 %collective-permute-start.11 = (f32[128,896]{1,0:T(8,128)S(1)}, f32[128,896]{1,0:T(8,128)S(1)}, u32[]{:S(2)}, u32[]{:S(2)}) collective-permute-start(f32[128,896]{1,0:T(8,128)S(1)} %collective-permute-done.10.refs_0_), channel_id=1, source_target_pairs={{1,0},{3,2},{5,4},{7,6},{9,8},{11,10},{13,12},{15,14},{17,16},{19,... | collective-permute-start | bytes 1376264 | tf_op jit(solution)/shard_map/ppermute | solution.py:354
  62.8 32.7 %collective-permute-start.5 = (f32[128,896]{1,0:T(8,128)S(1)}, f32[128,896]{1,0:T(8,128)S(1)}, u32[]{:S(2)}, u32[]{:S(2)}) collective-permute-start(f32[128,896]{1,0:T(8,128)S(1)} %collective-permute-done.4.refs_0_), channel_id=1, source_target_pairs={{1,0},{3,2},{5,4},{7,6},{9,8},{11,10},{13,12},{15,14},{17,16},{19,... | collective-permute-start | bytes 1376264 | tf_op jit(solution)/shard_map/ppermute | solution.py:354
  64.2 11.3 %collective-permute-start.14 = (f32[128,1024]{1,0:T(8,128)S(1)}, f32[128,1024]{1,0:T(8,128)S(1)}, u32[]{:S(2)}, u32[]{:S(2)}) collective-permute-start(f32[128,1024]{1,0:T(8,128)S(1)} %collective-permute-done.13.refs_0_), channel_id=1, source_target_pairs={{1,0},{3,2},{5,4},{7,6},{9,8},{11,10},{13,12},{15,14},{17,16},{19,... | collective-permute-start | bytes 1572872 | tf_op jit(solution)/shard_map/ppermute | solution.py:354
  65.5 8.4 %collective-permute-start.1 = (f32[128,384]{1,0:T(8,128)S(1)}, f32[128,384]{1,0:T(8,128)S(1)}, u32[]{:S(2)}, u32[]{:S(2)}) collective-permute-start(f32[128,384]{1,0:T(8,128)S(1)} %add_select_fusion.4), channel_id=1, source_target_pairs={{0,3},{1,4},{2,5},{3,6},{4,7},{5,8},{6,9},{7,10},{8,11},{9,12},{10... | collective-permute-start | bytes 589832 | tf_op jit(solution)/shard_map/ppermute | solution.py:353
  74.0 28.2 %collective-permute-start.2 = (f32[128,384]{1,0:T(8,128)S(1)}, f32[128,384]{1,0:T(8,128)S(1)}, u32[]{:S(2)}, u32[]{:S(2)}) collective-permute-start(f32[128,384]{1,0:T(8,128)S(1)} %collective-permute-done.1.refs_0_), channel_id=1, source_target_pairs={{1,0},{3,2},{5,4},{7,6},{9,8},{11,10},{13,12},{15,14},{17,16},{19,... | collective-permute-start | bytes 589832 | tf_op jit(solution)/shard_map/ppermute | solution.py:354
